TPU v7x, 1024 devices: a whole 4x4x32 slice. The times are simulated.
1024 devices in a mesh: frame: 16 (over z_hi, y, core), row: 16 (over z_lo), head: 4 (over x).
Axes of the slice: x: 4, y: 4, z: 32 (z_hi: 2, z_lo: 16; z = z_hi * 16 + z_lo), core: 2. Of those that a mesh axis runs over, the one named last changes fastest.
Arguments:
- queries: bfloat16 [32, 128, 16, 12, 128], P('frame', 'row', 'head'), may hold values from -6 to 6
- keys: bfloat16 [32, 128, 16, 12, 128], P('frame', 'row', 'head'), may hold values from -6 to 6
- values: bfloat16 [32, 128, 16, 12, 128], P('frame', 'row', 'head'), may hold values from -6 to 6
- out_grad: bfloat16 [32, 128, 16, 12, 128], P('frame', 'row', 'head'), may hold values from -6 to 6
- active: int32 [32, 16, 2, 27], replicated, may hold values from 0 to 1, as said below
Outputs:
- attended: bfloat16 [32, 128, 16, 12, 128], P('frame', 'row', 'head')
- query_grad: bfloat16 [32, 128, 16, 12, 128], P('frame', 'row', 'head')
- key_grad: bfloat16 [32, 128, 16, 12, 128], P('frame', 'row', 'head')
- value_grad: bfloat16 [32, 128, 16, 12, 128], P('frame', 'row', 'head')
Inputs may be any that keep to these rules, and one draw needn't show every extreme that they name: `active`: entry 13 (the tile with itself) is 1 for every tile; all other entries are 0 or 1.
All inputs are finite; a program needn't handle non-finite values.
Results may differ from a plain program's by a relative error of at most 0.011.
Values may be sent and summed in bfloat16 or wider, within the bound.
A program may use at most 32 MiB of HBM per device.

v0:
```python
import jax
import jax.numpy as jnp
from jax import lax
from jax.sharding import PartitionSpec as P

TF = 1
TR = 8
TC = 8


def padded(shard, sides, width):
    for axis, dim in sides:
        size, length = (lax.axis_size(axis), shard.shape[dim])
        up = [(i, (i + 1) % size) for i in range(size - 1)]
        down = [(j, i) for i, j in up]
        last = lax.slice_in_dim(shard, length - width, length, axis=dim)
        initial = lax.slice_in_dim(shard, 0, width, axis=dim)
        before = lax.ppermute(last, axis, up)
        after = lax.ppermute(initial, axis, down)
        shard = jnp.concatenate([before, shard, after], axis=dim)
    return shard


def product(form, left, right):
    return jnp.einsum(form, left, right, preferred_element_type=jnp.float32)


def slot_masks(act_ext, one_ext, frame_tiles, row_tiles, sign):
    col_tiles = act_ext.shape[2]
    own = jnp.arange(col_tiles, dtype=jnp.int32)[:, None]
    other = jnp.arange(col_tiles, dtype=jnp.int32)[None, :]
    offsets = jnp.arange(3, dtype=jnp.int32) - 1
    matches = (((other - own) * sign)[:, :, None] == offsets[None, None, :]).astype(jnp.float32)
    layers = []
    for offset in range(9):
        frame_step = offset // 3 - 1
        row_step = offset % 3 - 1
        if sign > 0:
            chosen = act_ext[1 : 1 + frame_tiles, 1 : 1 + row_tiles, :, 3 * offset : 3 * offset + 3]
            inside = one_ext[
                1 + frame_step : 1 + frame_step + frame_tiles,
                1 + row_step : 1 + row_step + row_tiles,
            ]
        else:
            chosen = act_ext[
                1 - frame_step : 1 - frame_step + frame_tiles,
                1 - row_step : 1 - row_step + row_tiles,
                :,
                3 * offset : 3 * offset + 3,
            ]
            inside = jnp.ones((frame_tiles, row_tiles), jnp.float32)
        layers.append(
            jnp.einsum("abio,ijo->abij", chosen.astype(jnp.float32), matches)
            * inside[:, :, None, None]
        )
    tiles = jnp.stack(layers, axis=3).reshape(frame_tiles, row_tiles, col_tiles, 9 * col_tiles)
    slab = TF * TR * col_tiles * TC
    query_pos = lax.broadcasted_iota(jnp.int32, (slab, col_tiles), 0)
    query_tile = lax.broadcasted_iota(jnp.int32, (slab, col_tiles), 1)
    query_cols = (query_pos % (col_tiles * TC) // TC == query_tile).astype(jnp.float32)
    key_pos = lax.broadcasted_iota(jnp.int32, (9 * col_tiles, 9 * slab), 1)
    key_tile = lax.broadcasted_iota(jnp.int32, (9 * col_tiles, 9 * slab), 0)
    key_code = key_pos // slab * col_tiles + key_pos % slab % (col_tiles * TC) // TC
    key_cols = (key_code == key_tile).astype(jnp.float32)
    spread_rows = jnp.einsum("qi,abik->abqk", query_cols, tiles)
    spread = jnp.einsum("abqj,jk->abqk", spread_rows, key_cols)
    return spread > 0.5


def gather_bands(wide, frame_tiles, row_tiles, sign):
    parts = []
    for offset in range(9):
        frame_step = sign * (offset // 3 - 1)
        row_step = sign * (offset % 3 - 1)
        parts.append(
            wide[
                1 + frame_step : 1 + frame_step + frame_tiles,
                1 + row_step : 1 + row_step + row_tiles,
            ]
        )
    stacked = jnp.stack(parts, axis=2)
    return stacked.reshape((frame_tiles, row_tiles, 9 * wide.shape[2]) + wide.shape[3:])


def query_side(query_slab, key_wide, value_wide, grad_slab, allowed, scaling):
    frame_tiles, row_tiles = (query_slab.shape[0], query_slab.shape[1])
    key_band = gather_bands(key_wide, frame_tiles, row_tiles, 1)
    value_band = gather_bands(value_wide, frame_tiles, row_tiles, 1)
    scores = product("abqd,abkd->abqk", query_slab, key_band) * scaling
    scores = jnp.where(allowed, scores, -jnp.inf)
    highest = jnp.max(scores, axis=-1, keepdims=True)
    log_total = highest + jnp.log(jnp.sum(jnp.exp(scores - highest), axis=-1, keepdims=True))
    weights = jnp.where(allowed, jnp.exp(scores - log_total), 0.0).astype(jnp.bfloat16)
    weights = lax.optimization_barrier(weights)
    attended = product("abqk,abkd->abqd", weights, value_band).astype(jnp.bfloat16)
    attended = lax.optimization_barrier(attended)
    grad_dot = jnp.sum(grad_slab.astype(jnp.float32) * attended.astype(jnp.float32), axis=-1)
    grad_probs = product("abqd,abkd->abqk", grad_slab, value_band)
    grad_scores = (
        weights.astype(jnp.float32) * (grad_probs - grad_dot[..., None]) * scaling
    ).astype(jnp.bfloat16)
    query_grad = product("abqk,abkd->abqd", grad_scores, key_band).astype(jnp.bfloat16)
    return (attended, query_grad, log_total[..., 0], grad_dot)


def key_side(key_slab, value_slab, query_wide, grad_wide, total_wide, dot_wide, allowed, scaling):
    frame_tiles, row_tiles = (key_slab.shape[0], key_slab.shape[1])
    query_band = gather_bands(query_wide, frame_tiles, row_tiles, -1)
    grad_band = gather_bands(grad_wide, frame_tiles, row_tiles, -1)
    total_band = gather_bands(total_wide, frame_tiles, row_tiles, -1)
    dot_band = gather_bands(dot_wide, frame_tiles, row_tiles, -1)
    scores = product("abkd,abqd->abkq", key_slab, query_band) * scaling
    weights = jnp.where(allowed, jnp.exp(scores - total_band[:, :, None, :]), 0.0).astype(
        jnp.bfloat16
    )
    weights = lax.optimization_barrier(weights)
    grad_probs = product("abkd,abqd->abkq", value_slab, grad_band)
    grad_scores = (
        weights.astype(jnp.float32) * (grad_probs - dot_band[:, :, None, :]) * scaling
    ).astype(jnp.bfloat16)
    key_grad = product("abkq,abqd->abkd", grad_scores, query_band).astype(jnp.bfloat16)
    value_grad = product("abkq,abqd->abkd", weights, grad_band).astype(jnp.bfloat16)
    return (key_grad, value_grad)


def on_device(queries, keys, values, out_grad, active):
    frames_here, rows_here, cols_here, heads_all, head_dim = queries.shape
    head_count = lax.axis_size("head")
    groups = heads_all // head_count
    columns = cols_here * head_count
    frame_tiles = frames_here // TF
    row_tiles = rows_here // TR
    scaling = head_dim ** (-0.5)
    frame_at = lax.axis_index("frame")
    row_at = lax.axis_index("row")
    padded_active = jnp.pad(active, ((1, 1), (1, 1), (0, 0), (0, 0)))
    padded_ones = jnp.pad(jnp.ones((active.shape[0], active.shape[1]), jnp.float32), 1)
    act_ext = lax.dynamic_slice(
        padded_active,
        (frame_at * frame_tiles, row_at * row_tiles, 0, 0),
        (frame_tiles + 2, row_tiles + 2, active.shape[2], active.shape[3]),
    )
    one_ext = lax.dynamic_slice(
        padded_ones, (frame_at * frame_tiles, row_at * row_tiles), (frame_tiles + 2, row_tiles + 2)
    )
    front_mask = slot_masks(act_ext, one_ext, frame_tiles, row_tiles, 1)
    back_mask = slot_masks(act_ext, one_ext, frame_tiles, row_tiles, -1)

    def split_heads(tensor):
        return tensor.reshape(frames_here, rows_here, cols_here, head_count, groups, head_dim)

    def to_slabs(tensor):
        count = tensor.shape[3]
        shaped = tensor.reshape(frame_tiles, TF, row_tiles, TR, columns, count, head_dim)
        return jnp.transpose(shaped, (5, 0, 2, 1, 3, 4, 6)).reshape(
            count, frame_tiles, row_tiles, TF * TR * columns, head_dim
        )

    def from_slabs(result):
        count = result.shape[0]
        shaped = result.reshape(count, frame_tiles, row_tiles, TF, TR, columns, head_dim)
        return jnp.transpose(shaped, (1, 3, 2, 4, 5, 0, 6)).reshape(
            frames_here, rows_here, columns, 1, count, head_dim
        )

    query_slab = to_slabs(
        lax.all_to_all(split_heads(queries), "head", split_axis=3, concat_axis=2, tiled=True)[
            :, :, :, 0
        ]
    )
    key_slab = to_slabs(
        lax.all_to_all(split_heads(keys), "head", split_axis=3, concat_axis=2, tiled=True)[
            :, :, :, 0
        ]
    )
    value_slab = to_slabs(
        lax.all_to_all(split_heads(values), "head", split_axis=3, concat_axis=2, tiled=True)[
            :, :, :, 0
        ]
    )
    grad_slab = to_slabs(
        lax.all_to_all(split_heads(out_grad), "head", split_axis=3, concat_axis=2, tiled=True)[
            :, :, :, 0
        ]
    )
    pair_rims = padded(jnp.stack([key_slab, value_slab]), (("frame", 2), ("row", 3)), 1)
    key_wide = pair_rims[0]
    value_wide = pair_rims[1]

    def front(parts):
        return query_side(parts[0], parts[1], parts[2], parts[3], front_mask, scaling)

    attended, query_grad, log_total, grad_dot = lax.map(
        front, (query_slab, key_wide, value_wide, grad_slab)
    )
    other_rims = padded(jnp.stack([query_slab, grad_slab]), (("frame", 2), ("row", 3)), 1)
    query_wide = other_rims[0]
    grad_wide = other_rims[1]
    stats = padded(jnp.stack([log_total, grad_dot]), (("frame", 2), ("row", 3)), 1)

    def back(parts):
        return key_side(
            parts[0], parts[1], parts[2], parts[3], parts[4], parts[5], back_mask, scaling
        )

    key_grad, value_grad = lax.map(
        back, (key_slab, value_slab, query_wide, grad_wide, stats[0], stats[1])
    )
    returned = (
        lax.all_to_all(from_slabs(attended), "head", split_axis=2, concat_axis=3, tiled=True),
        lax.all_to_all(from_slabs(query_grad), "head", split_axis=2, concat_axis=3, tiled=True),
        lax.all_to_all(from_slabs(key_grad), "head", split_axis=2, concat_axis=3, tiled=True),
        lax.all_to_all(from_slabs(value_grad), "head", split_axis=2, concat_axis=3, tiled=True),
    )
    return tuple(
        (
            tensor.reshape(frames_here, rows_here, cols_here, heads_all, head_dim)
            for tensor in returned
        )
    )


def solution(mesh):
    in_specs = (
        P("frame", "row", "head", None, None),
        P("frame", "row", "head", None, None),
        P("frame", "row", "head", None, None),
        P("frame", "row", "head", None, None),
        P(),
    )
    out_specs = (
        P("frame", "row", "head", None, None),
        P("frame", "row", "head", None, None),
        P("frame", "row", "head", None, None),
        P("frame", "row", "head", None, None),
    )
    return jax.shard_map(
        on_device, mesh=mesh, in_specs=in_specs, out_specs=out_specs, check_vma=False
    )
```

profile of v0, /device:TPU:25, one launch (start us, length us, event | category | flops | bytes accessed | tf_op | source)
XLA Modules:
  0.0 284.3 jit_solution(577043361498613961)
XLA Ops:
  0.6 1.7 copy.1013
  2.4 4.0 %all-to-all-start.1 = ((bf16[2,8,4,4,3,128]{5,2,4,1,0,3:T(4,128)(2,1)}), bf16[2,8,4,4,3,128]{5,2,4,1,0,3:T(4,128)(2,1)S(1)}, u32[]{:S(2)}, u32[]{:S(2)}) async-start(bf16[2,8,4,4,3,128]{5,2,4,1,0,3:T(4,128)(2,1)} %copy.1013), calls=%async_computation.1 | async-start | bytes 393216 | tf_op jit(solution)/shard_map/all_to_all | solution.py:172
  13.9 4.2 %all-to-all-start.2 = ((bf16[2,8,4,4,3,128]{5,2,4,1,0,3:T(4,128)(2,1)}), bf16[2,8,4,4,3,128]{5,2,4,1,0,3:T(4,128)(2,1)S(1)}, u32[]{:S(2)}, u32[]{:S(2)}) async-start(bf16[2,8,4,4,3,128]{5,2,4,1,0,3:T(4,128)(2,1)} %copy.1017), calls=%async_computation.2 | async-start | bytes 393216 | tf_op jit(solution)/shard_map/all_to_all | solution.py:177
  20.0 3.4 %all-to-all-done.2 = bf16[2,8,4,4,3,128]{5,2,4,1,0,3:T(4,128)(2,1)S(1)} async-done(((bf16[2,8,4,4,3,128]{5,2,4,1,0,3:T(4,128)(2,1)}), bf16[2,8,4,4,3,128]{5,2,4,1,0,3:T(4,128)(2,1)S(1)}, u32[]{:S(2)}, u32[]{:S(2)}) %all-to-all-start.2) | async-done | bytes 196640 | tf_op jit(solution)/shard_map/all_to_all | solution.py:177
  23.4 3.4 %all-to-all-start = ((bf16[2,8,4,4,3,128]{5,2,4,1,0,3:T(4,128)(2,1)}), bf16[2,8,4,4,3,128]{5,2,4,1,0,3:T(4,128)(2,1)S(1)}, u32[]{:S(2)}, u32[]{:S(2)}) async-start(bf16[2,8,4,4,3,128]{5,2,4,1,0,3:T(4,128)(2,1)} %copy.1009), calls=%async_computation | async-start | bytes 393216 | tf_op jit(solution)/shard_map/all_to_all | solution.py:167
  26.9 30.9 %collective-permute-start = (bf16[2,3,1,1,128,128]{5,4,2,1,3,0:T(8,128)(2,1)S(1)}, bf16[2,3,1,1,128,128]{5,4,2,1,3,0:T(8,128)(2,1)S(1)}, u32[]{:S(2)}, u32[]{:S(2)}) collective-permute-start(bf16[2,3,1,1,128,128]{5,4,2,1,3,0:T(8,128)(2,1)S(1)} %get-tuple-element.293), channel_id=1, source_target_pairs={{0,64},{64,128},{128,192},{192,256},{256,320},{320,384},{384,448},... | collective-permute-start | bytes 589832 | tf_op jit(solution)/shard_map/ppermute | solution.py:18
  57.8 1.9 collective-permute-start.1
  60.4 25.3 %collective-permute-done.1 = bf16[2,3,1,1,128,128]{5,4,2,1,3,0:T(8,128)(2,1)S(1)} collective-permute-done((bf16[2,3,1,1,128,128]{5,4,2,1,3,0:T(8,128)(2,1)S(1)}, bf16[2,3,1,1,128,128]{5,4,2,1,3,0:T(8,128)(2,1)S(1)}, u32[]{:S(2)}, u32[]{:S(2)}) %collective-permute-start.1) | collective-permute-done | bytes 196640 | tf_op jit(solution)/shard_map/ppermute | solution.py:19
  85.7 1.0 pad_maximum_fusion.2
  86.7 17.7 %collective-permute-start.2 = (bf16[2,3,4,1,128,128]{5,4,2,1,3,0:T(8,128)(2,1)}, bf16[2,3,4,1,128,128]{5,4,2,1,3,0:T(8,128)(2,1)S(1)}, u32[]{:S(2)}, u32[]{:S(2)}) collective-permute-start(bf16[2,3,4,1,128,128]{5,4,2,1,3,0:T(8,128)(2,1)} %pad_maximum_fusion.2), channel_id=1, source_target_pairs={{0,4},{4,8},{8,12},{12,16},{16,20},{20,24},{24,28},{28,32},{32,36}... | collective-permute-start | bytes 2359304 | tf_op jit(solution)/shard_map/ppermute | solution.py:18
  104.4 1.3 collective-permute-start.3
  105.7 4.6 %all-to-all-start.3 = ((bf16[2,8,4,4,3,128]{5,2,4,1,0,3:T(4,128)(2,1)}), bf16[2,8,4,4,3,128]{5,2,4,1,0,3:T(4,128)(2,1)S(1)}, u32[]{:S(2)}, u32[]{:S(2)}) async-start(bf16[2,8,4,4,3,128]{5,2,4,1,0,3:T(4,128)(2,1)} %copy.1021), calls=%async_computation.3 | async-start | bytes 393216 | tf_op jit(solution)/shard_map/all_to_all | solution.py:182
  110.9 4.6 %all-to-all-done.3 = bf16[2,8,4,4,3,128]{5,2,4,1,0,3:T(4,128)(2,1)S(1)} async-done(((bf16[2,8,4,4,3,128]{5,2,4,1,0,3:T(4,128)(2,1)}), bf16[2,8,4,4,3,128]{5,2,4,1,0,3:T(4,128)(2,1)S(1)}, u32[]{:S(2)}, u32[]{:S(2)}) %all-to-all-start.3) | async-done | bytes 196640 | tf_op jit(solution)/shard_map/all_to_all | solution.py:182
  116.2 1.7 fusion.107
  117.8 2.7 collective-permute-start.4
  120.5 1.9 collective-permute-start.5
  122.4 1.3 fusion.88
  123.7 24.7 %collective-permute-done.5 = bf16[2,3,1,1,128,128]{5,4,2,1,3,0:T(8,128)(2,1)S(1)} collective-permute-done((bf16[2,3,1,1,128,128]{5,4,2,1,3,0:T(8,128)(2,1)S(1)}, bf16[2,3,1,1,128,128]{5,4,2,1,3,0:T(8,128)(2,1)S(1)}, u32[]{:S(2)}, u32[]{:S(2)}) %collective-permute-start.5) | collective-permute-done | bytes 196640 | tf_op jit(solution)/shard_map/ppermute | solution.py:19
  148.5 2.0 pad_maximum_fusion.3
  150.4 15.7 %collective-permute-start.6 = (bf16[2,3,4,1,128,128]{5,4,2,1,3,0:T(8,128)(2,1)}, bf16[2,3,4,1,128,128]{5,4,2,1,3,0:T(8,128)(2,1)}, u32[]{:S(2)}, u32[]{:S(2)}) collective-permute-start(bf16[2,3,4,1,128,128]{5,4,2,1,3,0:T(8,128)(2,1)} %pad_maximum_fusion.3), channel_id=1, source_target_pairs={{0,4},{4,8},{8,12},{12,16},{16,20},{20,24},{24,28},{28,32},{32,36}... | collective-permute-start | bytes 2359304 | tf_op jit(solution)/shard_map/ppermute | solution.py:18
  166.1 1.3 collective-permute-start.7
  167.8 1.2 slice_bitcast_fusion.38
  170.4 19.2 %while.28 = (s32[]{:T(128)}, bf16[3,2,1,128,128]{4,3,1,2,0:T(8,128)(2,1)}, bf16[3,2,1,128,128]{4,3,1,2,0:T(8,128)(2,1)}, f32[3,2,1,128]{3,1,2,0:T(2,128)S(1)}, f...) while((s32[]{:T(128)}, ...), condition=%wide.region_4.5_spmd, body=%wide.region_0.4_spmd.sunk | while | flops 306019840 | bytes 12727937 | solution.py:193
  170.4 1.0 dynamic-slice_bitcast_fusion.9
  173.3 1.0 fusion.338
  174.2 2.0 fusion.339
  176.9 1.0 dynamic-slice_bitcast_fusion.9
  179.7 1.0 fusion.338
  180.6 2.0 fusion.339
  183.3 1.0 dynamic-slice_bitcast_fusion.9
  186.1 1.0 fusion.338
  187.0 2.0 fusion.339
  189.7 2.0 collective-permute-start.8
  191.7 2.3 collective-permute-start.9
  194.0 1.8 pad_maximum_fusion.1
  195.8 21.3 %collective-permute-done.9 = f32[2,3,1,1,128]{4,2,3,1,0:T(1,128)S(1)} collective-permute-done((f32[2,3,1,1,128]{4,2,3,1,0:T(1,128)S(1)}, f32[2,3,1,1,128]{4,2,3,1,0:T(1,128)S(1)}, u32[]{:S(2)}, u32[]{:S(2)}) %collective-permute-start.9) | collective-permute-done | bytes 3104 | tf_op jit(solution)/shard_map/ppermute | solution.py:19
  217.1 4.4 %collective-permute-start.10 = (f32[2,3,4,1,128]{4,2,3,1,0:T(4,128)S(1)}, f32[2,3,4,1,128]{4,2,3,1,0:T(4,128)S(1)}, u32[]{:S(2)}, u32[]{:S(2)}) collective-permute-start(f32[2,3,4,1,128]{4,2,3,1,0:T(4,128)S(1)} %pad_maximum_fusion.7), channel_id=1, source_target_pairs={{0,4},{4,8},{8,12},{12,16},{16,20},{20,24},{24,28},{28,32},{32,36}... | collective-permute-start | bytes 36872 | tf_op jit(solution)/shard_map/ppermute | solution.py:18
  221.5 1.3 collective-permute-start.11
  223.7 3.4 %all-to-all-start.4 = ((bf16[2,8,16,1,3,128]{5,1,0,4,3,2:T(8,128)(2,1)}), bf16[2,8,16,1,3,128]{5,1,0,4,3,2:T(8,128)(2,1)S(1)}, u32[]{:S(2)}, u32[]{:S(2)}) async-start(bf16[2,8,16,1,3,128]{5,1,0,4,3,2:T(8,128)(2,1)} %copy.1028), calls=%async_computation.4 | async-start | bytes 393216 | tf_op jit(solution)/shard_map/all_to_all | solution.py:210
  228.5 3.8 %all-to-all-done.4 = bf16[2,8,16,1,3,128]{5,1,0,4,3,2:T(8,128)(2,1)S(1)} async-done(((bf16[2,8,16,1,3,128]{5,1,0,4,3,2:T(8,128)(2,1)}), bf16[2,8,16,1,3,128]{5,1,0,4,3,2:T(8,128)(2,1)S(1)}, u32[]{:S(2)}, u32[]{:S(2)}) %all-to-all-start.4) | async-done | bytes 196640 | tf_op jit(solution)/shard_map/all_to_all | solution.py:210
  232.2 4.0 %all-to-all-start.5 = ((bf16[2,8,16,1,3,128]{5,1,0,4,3,2:T(8,128)(2,1)}), bf16[2,8,16,1,3,128]{5,1,0,4,3,2:T(8,128)(2,1)}, u32[]{:S(2)}, u32[]{:S(2)}) async-start(bf16[2,8,16,1,3,128]{5,1,0,4,3,2:T(8,128)(2,1)} %copy.1031), calls=%async_computation.5 | async-start | bytes 393216 | tf_op jit(solution)/shard_map/all_to_all | solution.py:211
  237.6 26.2 %while.29 = (s32[]{:T(128)}, bf16[3,2,1,128,128]{4,3,1,2,0:T(8,128)(2,1)}, bf16[3,2,1,128,128]{4,3,1,2,0:T(8,128)(2,1)}, pred[2,1,128,1152]{3,2,0,1:T(32,128)(4,...) while((s32[]{:T(128)}, ...), condition=%wide.region_6.7_spmd, body=%wide.region_5.6_spmd.sunk | while | flops 304709632 | bytes 11133073 | solution.py:206
  238.1 0.8 dynamic-slice_bitcast_fusion.11
  238.9 1.6 fusion.366
  240.5 0.9 fusion.369
  242.1 1.4 stack.283
  244.1 2.2 fusion.368
  246.8 0.8 dynamic-slice_bitcast_fusion.11
  247.6 1.6 fusion.366
  249.3 0.9 fusion.369
  250.8 1.4 stack.283
  252.9 2.2 fusion.368
  255.5 0.8 dynamic-slice_bitcast_fusion.11
  256.4 1.6 fusion.366
  258.0 0.9 fusion.369
  259.6 1.4 stack.283
  261.6 2.2 fusion.368
  263.9 1.7 copy.1061
  265.6 4.2 %all-to-all-start.6 = ((bf16[2,8,16,1,3,128]{5,1,0,4,3,2:T(8,128)(2,1)}), bf16[2,8,16,1,3,128]{5,1,0,4,3,2:T(8,128)(2,1)S(1)}, u32[]{:S(2)}, u32[]{:S(2)}) async-start(bf16[2,8,16,1,3,128]{5,1,0,4,3,2:T(8,128)(2,1)} %copy.1061), calls=%async_computation.6 | async-start | bytes 393216 | tf_op jit(solution)/shard_map/all_to_all | solution.py:212
  269.8 1.6 copy.1064
  271.4 3.5 %all-to-all-done.6 = bf16[2,8,16,1,3,128]{5,1,0,4,3,2:T(8,128)(2,1)S(1)} async-done(((bf16[2,8,16,1,3,128]{5,1,0,4,3,2:T(8,128)(2,1)}), bf16[2,8,16,1,3,128]{5,1,0,4,3,2:T(8,128)(2,1)S(1)}, u32[]{:S(2)}, u32[]{:S(2)}) %all-to-all-start.6) | async-done | bytes 196640 | tf_op jit(solution)/shard_map/all_to_all | solution.py:212
  274.9 3.4 %all-to-all-start.7 = ((bf16[2,8,16,1,3,128]{5,1,0,4,3,2:T(8,128)(2,1)}), bf16[2,8,16,1,3,128]{5,1,0,4,3,2:T(8,128)(2,1)S(1)}, u32[]{:S(2)}, u32[]{:S(2)}) async-start(bf16[2,8,16,1,3,128]{5,1,0,4,3,2:T(8,128)(2,1)} %copy.1064), calls=%async_computation.7 | async-start | bytes 393216 | tf_op jit(solution)/shard_map/all_to_all | solution.py:213
  279.2 1.0 copy.1032
  281.8 1.7 all-to-all-done.7
  (298 shorter events, 31.8 us)
Async XLA Ops:
  0.6 5.8 %copy-start.8 = (s32[32,16,2,27]{0,2,3,1:T(2,128)S(1)}, s32[32,16,2,27]{0,2,3,1:T(2,128)}, u32[]{:S(2)}) copy-start(s32[32,16,2,27]{0,2,3,1:T(2,128)} %param.13) | copy-start | bytes 331780
  2.4 11.6 %all-to-all-start.1 = ((bf16[2,8,4,4,3,128]{5,2,4,1,0,3:T(4,128)(2,1)}), bf16[2,8,4,4,3,128]{5,2,4,1,0,3:T(4,128)(2,1)S(1)}, u32[]{:S(2)}, u32[]{:S(2)}) async-start(bf16[2,8,4,4,3,128]{5,2,4,1,0,3:T(4,128)(2,1)} %copy.1013), calls=%async_computation.1 | async-start | bytes 393216 | tf_op jit(solution)/shard_map/all_to_all | solution.py:172
  6.4 3.8 %copy-start.9 = (bf16[2,8,4,12,128]{4,2,3,1,0:T(4,128)(2,1)S(1)}, bf16[2,8,4,12,128]{4,2,3,1,0:T(4,128)(2,1)}, u32[]{:S(2)}) copy-start(bf16[2,8,4,12,128]{4,2,3,1,0:T(4,128)(2,1)} %param.11) | copy-start | bytes 589828
  7.3 11.0 %copy-start.10 = (bf16[2,8,4,12,128]{4,2,3,1,0:T(4,128)(2,1)S(1)}, bf16[2,8,4,12,128]{4,2,3,1,0:T(4,128)(2,1)}, u32[]{:S(2)}) copy-start(bf16[2,8,4,12,128]{4,2,3,1,0:T(4,128)(2,1)} %param.9) | copy-start | bytes 589828
  8.0 11.1 %copy-start.11 = (bf16[2,8,4,12,128]{4,2,3,1,0:T(4,128)(2,1)S(1)}, bf16[2,8,4,12,128]{4,2,3,1,0:T(4,128)(2,1)}, u32[]{:S(2)}) copy-start(bf16[2,8,4,12,128]{4,2,3,1,0:T(4,128)(2,1)} %param.12) | copy-start | bytes 589828
  13.9 9.4 %all-to-all-start.2 = ((bf16[2,8,4,4,3,128]{5,2,4,1,0,3:T(4,128)(2,1)}), bf16[2,8,4,4,3,128]{5,2,4,1,0,3:T(4,128)(2,1)S(1)}, u32[]{:S(2)}, u32[]{:S(2)}) async-start(bf16[2,8,4,4,3,128]{5,2,4,1,0,3:T(4,128)(2,1)} %copy.1017), calls=%async_computation.2 | async-start | bytes 393216 | tf_op jit(solution)/shard_map/all_to_all | solution.py:177
  20.0 147.4 %copy-start = (bf16[3,2,1,1,8,16,128]{6,5,4,1,0,3,2:T(8,128)(2,1)}, bf16[3,2,1,1,8,16,128]{6,5,4,1,0,3,2:T(8,128)(2,1)S(1)}, u32[]{:S(2)}) copy-start(bf16[3,2,1,1,8,16,128]{6,5,4,1,0,3,2:T(8,128)(2,1)S(1)} %copy.1015) | copy-start | bytes 589828
  23.4 82.3 %all-to-all-start = ((bf16[2,8,4,4,3,128]{5,2,4,1,0,3:T(4,128)(2,1)}), bf16[2,8,4,4,3,128]{5,2,4,1,0,3:T(4,128)(2,1)S(1)}, u32[]{:S(2)}, u32[]{:S(2)}) async-start(bf16[2,8,4,4,3,128]{5,2,4,1,0,3:T(4,128)(2,1)} %copy.1009), calls=%async_computation | async-start | bytes 393216 | tf_op jit(solution)/shard_map/all_to_all | solution.py:167
  26.8 140.6 %copy-start.1 = (bf16[3,2,1,1,8,16,128]{6,5,4,1,0,3,2:T(8,128)(2,1)}, bf16[3,2,1,1,8,16,128]{6,5,4,1,0,3,2:T(8,128)(2,1)S(1)}, u32[]{:S(2)}) copy-start(bf16[3,2,1,1,8,16,128]{6,5,4,1,0,3,2:T(8,128)(2,1)S(1)} %copy.1019) | copy-start | bytes 589828
  26.9 33.5 %collective-permute-start = (bf16[2,3,1,1,128,128]{5,4,2,1,3,0:T(8,128)(2,1)S(1)}, bf16[2,3,1,1,128,128]{5,4,2,1,3,0:T(8,128)(2,1)S(1)}, u32[]{:S(2)}, u32[]{:S(2)}) collective-permute-start(bf16[2,3,1,1,128,128]{5,4,2,1,3,0:T(8,128)(2,1)S(1)} %get-tuple-element.293), channel_id=1, source_target_pairs={{0,64},{64,128},{128,192},{192,256},{256,320},{320,384},{384,448},... | collective-permute-start | bytes 589832 | tf_op jit(solution)/shard_map/ppermute | solution.py:18
  57.8 27.9 %collective-permute-start.1 = (bf16[2,3,1,1,128,128]{5,4,2,1,3,0:T(8,128)(2,1)S(1)}, bf16[2,3,1,1,128,128]{5,4,2,1,3,0:T(8,128)(2,1)S(1)}, u32[]{:S(2)}, u32[]{:S(2)}) collective-permute-start(bf16[2,3,1,1,128,128]{5,4,2,1,3,0:T(8,128)(2,1)S(1)} %get-tuple-element.294), channel_id=1, source_target_pairs={{64,0},{128,64},{192,128},{256,192},{320,256},{384,320},{448,384},... | collective-permute-start | bytes 589832 | tf_op jit(solution)/shard_map/ppermute | solution.py:19
  86.7 80.7 %collective-permute-start.2 = (bf16[2,3,4,1,128,128]{5,4,2,1,3,0:T(8,128)(2,1)}, bf16[2,3,4,1,128,128]{5,4,2,1,3,0:T(8,128)(2,1)S(1)}, u32[]{:S(2)}, u32[]{:S(2)}) collective-permute-start(bf16[2,3,4,1,128,128]{5,4,2,1,3,0:T(8,128)(2,1)} %pad_maximum_fusion.2), channel_id=1, source_target_pairs={{0,4},{4,8},{8,12},{12,16},{16,20},{20,24},{24,28},{28,32},{32,36}... | collective-permute-start | bytes 2359304 | tf_op jit(solution)/shard_map/ppermute | solution.py:18
  104.4 63.1 %collective-permute-start.3 = (bf16[2,3,4,1,128,128]{5,4,2,1,3,0:T(8,128)(2,1)}, bf16[2,3,4,1,128,128]{5,4,2,1,3,0:T(8,128)(2,1)S(1)}, u32[]{:S(2)}, u32[]{:S(2)}) collective-permute-start(bf16[2,3,4,1,128,128]{5,4,2,1,3,0:T(8,128)(2,1)} %pad_maximum_fusion.2), channel_id=1, source_target_pairs={{4,0},{8,4},{12,8},{16,12},{20,16},{24,20},{28,24},{32,28},{36,32}... | collective-permute-start | bytes 2359304 | tf_op jit(solution)/shard_map/ppermute | solution.py:19
  105.7 9.8 %all-to-all-start.3 = ((bf16[2,8,4,4,3,128]{5,2,4,1,0,3:T(4,128)(2,1)}), bf16[2,8,4,4,3,128]{5,2,4,1,0,3:T(4,128)(2,1)S(1)}, u32[]{:S(2)}, u32[]{:S(2)}) async-start(bf16[2,8,4,4,3,128]{5,2,4,1,0,3:T(4,128)(2,1)} %copy.1021), calls=%async_computation.3 | async-start | bytes 393216 | tf_op jit(solution)/shard_map/all_to_all | solution.py:182
  117.8 5.9 %collective-permute-start.4 = (bf16[2,3,1,1,128,128]{5,4,2,1,3,0:T(8,128)(2,1)}, bf16[2,3,1,1,128,128]{5,4,2,1,3,0:T(8,128)(2,1)S(1)}, u32[]{:S(2)}, u32[]{:S(2)}) collective-permute-start(bf16[2,3,1,1,128,128]{5,4,2,1,3,0:T(8,128)(2,1)} %get-tuple-element.291), channel_id=1, source_target_pairs={{0,64},{64,128},{128,192},{192,256},{256,320},{320,384},{384,448},... | collective-permute-start | bytes 589832 | tf_op jit(solution)/shard_map/ppermute | solution.py:18
  120.5 27.9 %collective-permute-start.5 = (bf16[2,3,1,1,128,128]{5,4,2,1,3,0:T(8,128)(2,1)S(1)}, bf16[2,3,1,1,128,128]{5,4,2,1,3,0:T(8,128)(2,1)S(1)}, u32[]{:S(2)}, u32[]{:S(2)}) collective-permute-start(bf16[2,3,1,1,128,128]{5,4,2,1,3,0:T(8,128)(2,1)S(1)} %get-tuple-element.292), channel_id=1, source_target_pairs={{64,0},{128,64},{192,128},{256,192},{320,256},{384,320},{448,384},... | collective-permute-start | bytes 589832 | tf_op jit(solution)/shard_map/ppermute | solution.py:19
  123.7 43.7 %copy-start.2 = (bf16[2,3,1,1,128,128]{5,4,2,1,3,0:T(8,128)(2,1)}, bf16[2,3,1,1,128,128]{5,4,2,1,3,0:T(8,128)(2,1)S(1)}, u32[]{:S(2)}) copy-start(bf16[2,3,1,1,128,128]{5,4,2,1,3,0:T(8,128)(2,1)S(1)} %collective-permute-done.4) | copy-start | bytes 589828
  148.5 19.0 %copy-start.3 = (bf16[2,3,1,1,128,128]{5,4,2,1,3,0:T(8,128)(2,1)}, bf16[2,3,1,1,128,128]{5,4,2,1,3,0:T(8,128)(2,1)S(1)}, u32[]{:S(2)}) copy-start(bf16[2,3,1,1,128,128]{5,4,2,1,3,0:T(8,128)(2,1)S(1)} %collective-permute-done.5) | copy-start | bytes 589828
  150.4 43.6 %collective-permute-start.6 = (bf16[2,3,4,1,128,128]{5,4,2,1,3,0:T(8,128)(2,1)}, bf16[2,3,4,1,128,128]{5,4,2,1,3,0:T(8,128)(2,1)}, u32[]{:S(2)}, u32[]{:S(2)}) collective-permute-start(bf16[2,3,4,1,128,128]{5,4,2,1,3,0:T(8,128)(2,1)} %pad_maximum_fusion.3), channel_id=1, source_target_pairs={{0,4},{4,8},{8,12},{12,16},{16,20},{20,24},{24,28},{28,32},{32,36}... | collective-permute-start | bytes 2359304 | tf_op jit(solution)/shard_map/ppermute | solution.py:18
  166.1 27.9 %collective-permute-start.7 = (bf16[2,3,4,1,128,128]{5,4,2,1,3,0:T(8,128)(2,1)}, bf16[2,3,4,1,128,128]{5,4,2,1,3,0:T(8,128)(2,1)}, u32[]{:S(2)}, u32[]{:S(2)}) collective-permute-start(bf16[2,3,4,1,128,128]{5,4,2,1,3,0:T(8,128)(2,1)} %pad_maximum_fusion.3), channel_id=1, source_target_pairs={{4,0},{8,4},{12,8},{16,12},{20,16},{24,20},{28,24},{32,28},{36,32}... | collective-permute-start | bytes 2359304 | tf_op jit(solution)/shard_map/ppermute | solution.py:19
  189.7 6.1 %collective-permute-start.8 = (f32[2,3,1,1,128]{4,2,3,1,0:T(1,128)S(1)}, f32[2,3,1,1,128]{4,2,3,1,0:T(1,128)S(1)}, u32[]{:S(2)}, u32[]{:S(2)}) collective-permute-start(f32[2,3,1,1,128]{4,2,3,1,0:T(1,128)S(1)} %get-tuple-element.297), channel_id=1, source_target_pairs={{0,64},{64,128},{128,192},{192,256},{256,320},{320,384},{384,448},... | collective-permute-start | bytes 9224 | tf_op jit(solution)/shard_map/ppermute | solution.py:18
  191.7 25.4 %collective-permute-start.9 = (f32[2,3,1,1,128]{4,2,3,1,0:T(1,128)S(1)}, f32[2,3,1,1,128]{4,2,3,1,0:T(1,128)S(1)}, u32[]{:S(2)}, u32[]{:S(2)}) collective-permute-start(f32[2,3,1,1,128]{4,2,3,1,0:T(1,128)S(1)} %get-tuple-element.298), channel_id=1, source_target_pairs={{64,0},{128,64},{192,128},{256,192},{320,256},{384,320},{448,384},... | collective-permute-start | bytes 9224 | tf_op jit(solution)/shard_map/ppermute | solution.py:19
  217.1 5.9 %copy-start.6 = (bf16[3,2,1,128,128]{4,3,1,2,0:T(8,128)(2,1)S(1)}, bf16[3,2,1,128,128]{4,3,1,2,0:T(8,128)(2,1)}, u32[]{:S(2)}) copy-start(bf16[3,2,1,128,128]{4,3,1,2,0:T(8,128)(2,1)} %get-tuple-element.112) | copy-start | bytes 589828
  217.1 10.0 %copy-start.7 = (bf16[3,2,1,128,128]{4,3,1,2,0:T(8,128)(2,1)S(1)}, bf16[3,2,1,128,128]{4,3,1,2,0:T(8,128)(2,1)}, u32[]{:S(2)}) copy-start(bf16[3,2,1,128,128]{4,3,1,2,0:T(8,128)(2,1)} %get-tuple-element.113) | copy-start | bytes 589828
  217.1 10.7 %collective-permute-start.10 = (f32[2,3,4,1,128]{4,2,3,1,0:T(4,128)S(1)}, f32[2,3,4,1,128]{4,2,3,1,0:T(4,128)S(1)}, u32[]{:S(2)}, u32[]{:S(2)}) collective-permute-start(f32[2,3,4,1,128]{4,2,3,1,0:T(4,128)S(1)} %pad_maximum_fusion.7), channel_id=1, source_target_pairs={{0,4},{4,8},{8,12},{12,16},{16,20},{20,24},{24,28},{28,32},{32,36}... | collective-permute-start | bytes 36872 | tf_op jit(solution)/shard_map/ppermute | solution.py:18
  221.5 6.3 %collective-permute-start.11 = (f32[2,3,4,1,128]{4,2,3,1,0:T(4,128)S(1)}, f32[2,3,4,1,128]{4,2,3,1,0:T(4,128)S(1)}, u32[]{:S(2)}, u32[]{:S(2)}) collective-permute-start(f32[2,3,4,1,128]{4,2,3,1,0:T(4,128)S(1)} %pad_maximum_fusion.7), channel_id=1, source_target_pairs={{4,0},{8,4},{12,8},{16,12},{20,16},{24,20},{28,24},{32,28},{36,32}... | collective-permute-start | bytes 36872 | tf_op jit(solution)/shard_map/ppermute | solution.py:19
  223.7 8.5 %all-to-all-start.4 = ((bf16[2,8,16,1,3,128]{5,1,0,4,3,2:T(8,128)(2,1)}), bf16[2,8,16,1,3,128]{5,1,0,4,3,2:T(8,128)(2,1)S(1)}, u32[]{:S(2)}, u32[]{:S(2)}) async-start(bf16[2,8,16,1,3,128]{5,1,0,4,3,2:T(8,128)(2,1)} %copy.1028), calls=%async_computation.4 | async-start | bytes 393216 | tf_op jit(solution)/shard_map/all_to_all | solution.py:210
  232.2 5.4 %copy-start.4 = (bf16[2,8,16,1,3,128]{5,1,0,4,3,2:T(8,128)(2,1)}, bf16[2,8,16,1,3,128]{5,1,0,4,3,2:T(8,128)(2,1)S(1)}, u32[]{:S(2)}) copy-start(bf16[2,8,16,1,3,128]{5,1,0,4,3,2:T(8,128)(2,1)S(1)} %all-to-all-done.4) | copy-start | bytes 589828
  232.2 33.3 %all-to-all-start.5 = ((bf16[2,8,16,1,3,128]{5,1,0,4,3,2:T(8,128)(2,1)}), bf16[2,8,16,1,3,128]{5,1,0,4,3,2:T(8,128)(2,1)}, u32[]{:S(2)}, u32[]{:S(2)}) async-start(bf16[2,8,16,1,3,128]{5,1,0,4,3,2:T(8,128)(2,1)} %copy.1031), calls=%async_computation.5 | async-start | bytes 393216 | tf_op jit(solution)/shard_map/all_to_all | solution.py:211
  238.0 0.8 copy-start.12
  246.8 0.8 copy-start.12
  255.5 0.8 copy-start.12
  263.9 14.5 %copy-start.5 = (bf16[2,8,16,1,3,128]{5,1,0,4,3,2:T(8,128)(2,1)S(1)}, bf16[2,8,16,1,3,128]{5,1,0,4,3,2:T(8,128)(2,1)}, u32[]{:S(2)}) copy-start(bf16[2,8,16,1,3,128]{5,1,0,4,3,2:T(8,128)(2,1)} %copy-done.4) | copy-start | bytes 589828
  265.6 9.4 %all-to-all-start.6 = ((bf16[2,8,16,1,3,128]{5,1,0,4,3,2:T(8,128)(2,1)}), bf16[2,8,16,1,3,128]{5,1,0,4,3,2:T(8,128)(2,1)S(1)}, u32[]{:S(2)}, u32[]{:S(2)}) async-start(bf16[2,8,16,1,3,128]{5,1,0,4,3,2:T(8,128)(2,1)} %copy.1061), calls=%async_computation.6 | async-start | bytes 393216 | tf_op jit(solution)/shard_map/all_to_all | solution.py:212
  274.9 8.5 %all-to-all-start.7 = ((bf16[2,8,16,1,3,128]{5,1,0,4,3,2:T(8,128)(2,1)}), bf16[2,8,16,1,3,128]{5,1,0,4,3,2:T(8,128)(2,1)S(1)}, u32[]{:S(2)}, u32[]{:S(2)}) async-start(bf16[2,8,16,1,3,128]{5,1,0,4,3,2:T(8,128)(2,1)} %copy.1064), calls=%async_computation.7 | async-start | bytes 393216 | tf_op jit(solution)/shard_map/all_to_all | solution.py:213
where the time goes:
time: 287 us; the launch traced here: 284 us
  starting transfers between devices  114 us (40%)
  waiting for transfers between devices  88.9 us (31%)
  local copies, waits for them, and re-layouts  39.4 us (14%)
  matrix products  27.8 us (10%)
  other arithmetic  11.9 us (4%)
    ppermute x6, starting transfers between devices, padded(): before = lax.ppermute(last, axis, up)  73.3 us
    ppermute x6, waiting for transfers between devices, padded(): after = lax.ppermute(initial, axis, down)  71.3 us
    dot_general x18, matrix products, product(): return jnp.einsum(form, left, right, preferred_element_type=jnp.float32)  22.6 us
    ppermute x6, starting transfers between devices, padded(): after = lax.ppermute(initial, axis, down)  9.99 us
  transfers between devices with their start and end apart: 20, of which 9 were waited for; matrix products, arithmetic and copies ran while one was open for 27% of the time, Pallas kernels for 0%

commit v1 on v0

v1 whole, which is shorter than its diff:
```python
import functools
import math

import jax
import jax.numpy as jnp
from jax import lax
from jax.experimental import pallas as pl
from jax.experimental.pallas import tpu as pltpu
from jax.sharding import PartitionSpec as P

MESH = pl.DeviceIdType.MESH
NEG = -1e30
KEY, VAL, QRY, GRD = 0, 1, 2, 3
SLOTS = 27


def nt(left, right):
    return lax.dot_general(
        left, right, (((1,), (1,)), ((), ())), preferred_element_type=jnp.float32
    )


def nn(left, right):
    return jnp.dot(left, right, preferred_element_type=jnp.float32)


def tile_kernel(sizes, bias, k_in, v_in, q_in, g_in, *refs):
    frames, rows, heads, groups, scaling = sizes
    outs, refs = refs[:4], refs[4:]
    land, pack, wide, stats, own, back = refs[:6]
    in_sem, a_send, a_recv, z_send, z_recv, c_send, c_recv, d_send, d_recv = refs[6:15]
    o_send, o_recv, out_sem = refs[15:18]
    ins = (k_in, v_in, q_in, g_in)
    heads_all = groups * heads
    tall = heads_all * 16

    f_at = lax.axis_index("frame")
    r_at = lax.axis_index("row")
    x_at = lax.axis_index("head")
    up, down = f_at < frames - 1, f_at > 0
    right, left = r_at < rows - 1, r_at > 0
    far_up, far_down = f_at == frames // 2 - 1, f_at == frames // 2
    peers = [lax.rem(x_at + k, heads) for k in range(heads)]
    froms = [lax.rem(x_at + heads - k, heads) for k in range(heads)]

    def loading(t):
        return pltpu.make_async_copy(ins[t], land.at[t], in_sem.at[t])

    for t in range(4):
        loading(t).start()

    barrier = pltpu.get_barrier_semaphore()

    def greet(frame, row, head):
        pl.semaphore_signal(barrier, inc=1, device_id=(frame, row, head), device_id_type=MESH)

    for k in range(1, heads):
        greet(f_at, r_at, peers[k])
    pl.when(right)(lambda: greet(f_at, r_at + 1, x_at))
    pl.when(left)(lambda: greet(f_at, r_at - 1, x_at))
    pl.when(up)(lambda: greet(f_at + 1, r_at, x_at))
    pl.when(down)(lambda: greet(f_at - 1, r_at, x_at))

    @pl.when(jnp.logical_not(left))
    def _():
        wide[:, :, :, 0] = jnp.zeros_like(wide[:, :, :, 0])
        stats[:, :, 0] = jnp.zeros_like(stats[:, :, 0])

    @pl.when(jnp.logical_not(right))
    def _():
        wide[:, :, :, 2] = jnp.zeros_like(wide[:, :, :, 2])
        stats[:, :, 2] = jnp.zeros_like(stats[:, :, 2])

    @pl.when(jnp.logical_not(down))
    def _():
        wide[:, :, 0] = jnp.zeros_like(wide[:, :, 0])
        stats[:, 0] = jnp.zeros_like(stats[:, 0])

    @pl.when(jnp.logical_not(up))
    def _():
        wide[:, :, 3] = jnp.zeros_like(wide[:, :, 3])
        stats[:, 3] = jnp.zeros_like(stats[:, 3])

    out_row = lax.broadcasted_iota(jnp.int32, (tall, tall), 0)
    in_row = lax.broadcasted_iota(jnp.int32, (tall, tall), 1)

    def swapped(row):
        return ((row % 16) // 4) * (4 * heads_all) + (row // 16) * 4 + row % 4

    to_heads = (swapped(out_row) == in_row).astype(jnp.bfloat16)
    to_rows = (swapped(in_row) == out_row).astype(jnp.bfloat16)

    def exchange(t, k):
        there = peers[k]
        return pltpu.make_async_remote_copy(
            src_ref=pack.at[t, pl.ds(there * groups, groups)],
            dst_ref=wide.at[t, :, pl.ds(1, 2), 1, pl.ds(pl.multiple_of(x_at * 32, 32), 32)],
            send_sem=a_send.at[t, k - 1],
            recv_sem=a_recv.at[t, k - 1],
            device_id=(f_at, r_at, there),
            device_id_type=MESH,
        )

    def arriving(t, k):
        spot = pl.ds(pl.multiple_of(froms[k] * 32, 32), 32)
        return pltpu.make_async_remote_copy(
            src_ref=pack.at[t, pl.ds(0, groups)],
            dst_ref=wide.at[t, :, pl.ds(1, 2), 1, spot],
            send_sem=a_send.at[t, k - 1],
            recv_sem=a_recv.at[t, k - 1],
            device_id=(f_at, r_at, froms[k]),
            device_id_type=MESH,
        )

    def block(t, frame, row):
        ref = stats if t == 4 else wide.at[t]
        return ref.at[:, frame, row]

    def pair(t, row):
        ref = stats if t == 4 else wide.at[t]
        return ref.at[:, pl.ds(1, 2), row]

    def hop(src, dst, ss, rs, frame, row):
        return pltpu.make_async_remote_copy(
            src_ref=src,
            dst_ref=dst,
            send_sem=ss,
            recv_sem=rs,
            device_id=(frame, row, x_at),
            device_id_type=MESH,
        )

    def to_right(t):
        return hop(pair(t, 1), pair(t, 0), z_send.at[t, 0], z_recv.at[t, 0], f_at, r_at + 1)

    def to_left(t):
        return hop(pair(t, 1), pair(t, 2), z_send.at[t, 1], z_recv.at[t, 1], f_at, r_at - 1)

    def to_up(t):
        return hop(block(t, 2, 1), block(t, 0, 1), c_send.at[t, 0], c_recv.at[t, 0], f_at + 1, r_at)

    def to_down(t):
        return hop(block(t, 1, 1), block(t, 3, 1), c_send.at[t, 1], c_recv.at[t, 1], f_at - 1, r_at)

    def side_up(t, row):
        sem = 0 if row == 0 else 1
        return hop(
            block(t, 2, row), block(t, 0, row), d_send.at[t, sem], d_recv.at[t, sem], f_at + 1, r_at
        )

    def side_down(t, row):
        sem = 2 if row == 0 else 3
        return hop(
            block(t, 1, row), block(t, 3, row), d_send.at[t, sem], d_recv.at[t, sem], f_at - 1, r_at
        )

    def along_right(t, frame):
        sem = 0 if frame == 0 else 2
        return hop(
            block(t, frame, 1), block(t, frame, 0), d_send.at[t, sem], d_recv.at[t, sem], f_at, r_at + 1
        )

    def along_left(t, frame):
        sem = 1 if frame == 0 else 3
        return hop(
            block(t, frame, 1), block(t, frame, 2), d_send.at[t, sem], d_recv.at[t, sem], f_at, r_at - 1
        )

    both = jnp.logical_and
    near_up = both(up, jnp.logical_not(far_up))
    near_down = both(down, jnp.logical_not(far_down))

    def first_halo(t):
        pl.when(up)(lambda: to_up(t).start())
        pl.when(down)(lambda: to_down(t).start())
        pl.when(right)(lambda: to_right(t).start())
        pl.when(left)(lambda: to_left(t).start())

    def second_halo(t):
        pl.when(left)(lambda: to_right(t).wait_recv())
        pl.when(right)(lambda: to_left(t).wait_recv())
        pl.when(both(near_up, left))(lambda: side_up(t, 0).start())
        pl.when(both(near_up, right))(lambda: side_up(t, 2).start())
        pl.when(both(near_down, left))(lambda: side_down(t, 0).start())
        pl.when(both(near_down, right))(lambda: side_down(t, 2).start())
        pl.when(down)(lambda: to_up(t).wait_recv())
        pl.when(up)(lambda: to_down(t).wait_recv())
        pl.when(both(far_down, right))(lambda: along_right(t, 0).start())
        pl.when(both(far_down, left))(lambda: along_left(t, 0).start())
        pl.when(both(far_up, right))(lambda: along_right(t, 3).start())
        pl.when(both(far_up, left))(lambda: along_left(t, 3).start())

    def last_halo(t):
        pl.when(both(down, left))(lambda: side_up(t, 0).wait_recv())
        pl.when(both(down, right))(lambda: side_up(t, 2).wait_recv())
        pl.when(both(up, left))(lambda: side_down(t, 0).wait_recv())
        pl.when(both(up, right))(lambda: side_down(t, 2).wait_recv())

    def halo_sent(t):
        pl.when(up)(lambda: to_up(t).wait_send())
        pl.when(down)(lambda: to_down(t).wait_send())
        pl.when(right)(lambda: to_right(t).wait_send())
        pl.when(left)(lambda: to_left(t).wait_send())
        pl.when(both(near_up, left))(lambda: side_up(t, 0).wait_send())
        pl.when(both(near_up, right))(lambda: side_up(t, 2).wait_send())
        pl.when(both(near_down, left))(lambda: side_down(t, 0).wait_send())
        pl.when(both(near_down, right))(lambda: side_down(t, 2).wait_send())
        pl.when(both(far_down, right))(lambda: along_right(t, 0).wait_send())
        pl.when(both(far_down, left))(lambda: along_left(t, 0).wait_send())
        pl.when(both(far_up, right))(lambda: along_right(t, 3).wait_send())
        pl.when(both(far_up, left))(lambda: along_left(t, 3).wait_send())

    for t in range(4):
        loading(t).wait()
        for g in range(4):
            part = nn(to_heads, land[t, pl.ds(g * tall, tall)]).astype(jnp.bfloat16)
            pack[t, :, g // 2, pl.ds(16 * (g % 2), 16)] = part.reshape(heads_all, 16, 128)
        if t == 0:
            known = [right, left, up, down]
            pl.semaphore_wait(barrier, heads - 1 + sum(c.astype(jnp.int32) for c in known))
        for k in range(1, heads):
            exchange(t, k).start()
        wide[t, :, pl.ds(1, 2), 1, pl.ds(pl.multiple_of(x_at * 32, 32), 32)] = pack[
            t, pl.ds(x_at * groups, groups)
        ]

    def gathered(t):
        for k in range(1, heads):
            arriving(t, k).wait_recv()

    gathered(KEY)
    first_halo(KEY)
    gathered(VAL)
    first_halo(VAL)
    second_halo(KEY)
    gathered(QRY)
    first_halo(QRY)
    second_halo(VAL)
    gathered(GRD)
    first_halo(GRD)
    second_halo(QRY)
    second_halo(GRD)
    last_halo(KEY)
    last_halo(VAL)

    lanes = lax.broadcasted_iota(jnp.int32, (1, 128), 1)
    lane_grid = lax.broadcasted_iota(jnp.int32, (128, 128), 1)
    power = scaling * math.log2(math.e)

    def entry(i, j, l, slot):
        return bias[((i * 3 + j) * 2 + l) * SLOTS + slot]

    def query_step(i, carry):
        h, f = i // 2, i % 2
        q = wide[QRY, h, f + 1, 1]
        g = wide[GRD, h, f + 1, 1]
        k_band = wide[KEY, h, pl.ds(f, 3)].reshape(9 * 128, 128)
        v_band = wide[VAL, h, pl.ds(f, 3)].reshape(9 * 128, 128)
        masks = []
        for l in range(2):
            cells = []
            for a in range(3):
                for b in range(3):
                    frame = 2 * f_at + f + a - 1
                    row = r_at + b - 1
                    inside = (frame >= 0) & (frame < 2 * frames) & (row >= 0) & (row < rows)
                    pieces = []
                    for m in range(2):
                        value = entry(f + 1, 1, l, 9 * a + 3 * b + m - l + 1)
                        pieces.append(jnp.where(inside, value, NEG))
                    cells.append(jnp.where(lanes < 64, pieces[0], pieces[1]))
            masks.append(jnp.concatenate(cells, axis=1))
        mask = jnp.concatenate([m[None] for m in masks], axis=0)
        s = nt(q, k_band)
        s = (s.reshape(2, 64, 9 * 128) + mask).reshape(128, 9 * 128)
        top = jnp.max(s, axis=1, keepdims=True)
        p = jnp.exp2((s - top) * power)
        total = jnp.sum(p, axis=1, keepdims=True)
        inverse = 1.0 / total
        out = (nn(p.astype(jnp.bfloat16), v_band) * inverse).astype(jnp.bfloat16)
        own[0, h, f] = out
        dot = jnp.sum(g.astype(jnp.float32) * out.astype(jnp.float32), axis=1, keepdims=True)
        dp = nt(g, v_band)
        ds = (p * (dp - dot)).astype(jnp.bfloat16)
        own[1, h, f] = (nn(ds, k_band) * (inverse * scaling)).astype(jnp.bfloat16)
        level = top * power + jnp.log2(total)
        both_stats = jnp.where(lane_grid == 0, level, dot)
        stats[h, f + 1, 1] = both_stats.T[0:8]
        return carry

    lax.fori_loop(0, groups * 2, query_step, 0)

    def giving(o, k):
        spot = pl.ds(pl.multiple_of(peers[k] * 32, 32), 32)
        return pltpu.make_async_remote_copy(
            src_ref=own.at[o, :, :, spot],
            dst_ref=back.at[o, pl.ds(x_at * groups, groups)],
            send_sem=o_send.at[o, k - 1],
            recv_sem=o_recv.at[o, k - 1],
            device_id=(f_at, r_at, peers[k]),
            device_id_type=MESH,
        )

    def taking(o, k):
        return pltpu.make_async_remote_copy(
            src_ref=own.at[o, :, :, pl.ds(0, 32)],
            dst_ref=back.at[o, pl.ds(froms[k] * groups, groups)],
            send_sem=o_send.at[o, k - 1],
            recv_sem=o_recv.at[o, k - 1],
            device_id=(f_at, r_at, froms[k]),
            device_id_type=MESH,
        )

    def give(o):
        for k in range(1, heads):
            giving(o, k).start()
        spot = pl.ds(pl.multiple_of(x_at * 32, 32), 32)
        back[o, pl.ds(x_at * groups, groups)] = own[o, :, :, spot]

    def storing(o):
        return pltpu.make_async_copy(land.at[o], outs[o], out_sem.at[o])

    def finish(o):
        for k in range(1, heads):
            taking(o, k).wait_recv()
        for g in range(4):
            part = back[o, :, g // 2, pl.ds(16 * (g % 2), 16)].reshape(tall, 128)
            land[o, pl.ds(g * tall, tall)] = nn(to_rows, part).astype(jnp.bfloat16)
        storing(o).start()

    first_halo(4)
    give(0)
    give(1)
    second_halo(4)
    last_halo(QRY)
    last_halo(GRD)
    finish(0)
    finish(1)
    last_halo(4)

    def key_step(i, carry):
        h, f = i // 2, i % 2
        k = wide[KEY, h, f + 1, 1]
        v = wide[VAL, h, f + 1, 1]
        q_band = wide[QRY, h, pl.ds(f, 3)].reshape(9 * 128, 128)
        g_band = wide[GRD, h, pl.ds(f, 3)].reshape(9 * 128, 128)
        shifts, dots = [[], []], []
        for a in range(3):
            for b in range(3):
                pack_here = stats[h, f + a, b]
                level, dot = pack_here[0:1], pack_here[1:2]
                dots.append(dot)
                for l in range(2):
                    pieces = [
                        entry(f + a, b, l, 9 * (2 - a) + 3 * (2 - b) + l - m + 1) for m in range(2)
                    ]
                    shifts[l].append(jnp.where(lanes < 64, pieces[0], pieces[1]) - level)
        shift = jnp.concatenate([jnp.concatenate(s, axis=1)[None] for s in shifts], axis=0)
        dot_row = jnp.concatenate(dots, axis=1)
        s = nt(k, q_band) * power
        p = jnp.exp2(s.reshape(2, 64, 9 * 128) + shift).reshape(128, 9 * 128)
        own[3, h, f] = nn(p.astype(jnp.bfloat16), g_band).astype(jnp.bfloat16)
        dp = nt(v, g_band)
        ds = (p * (dp - dot_row)).astype(jnp.bfloat16)
        own[2, h, f] = (nn(ds, q_band) * scaling).astype(jnp.bfloat16)
        return carry

    lax.fori_loop(0, groups * 2, key_step, 0)
    give(2)
    give(3)
    finish(2)
    finish(3)

    for t in range(4):
        for k in range(1, heads):
            exchange(t, k).wait_send()
            giving(t, k).wait_send()
    for t in range(5):
        halo_sent(t)
    for o in range(4):
        storing(o).wait()


def on_device(sizes, queries, keys, values, out_grad, active):
    frames, rows, heads, groups, scaling = sizes
    frames_here, rows_here, cols_here, heads_all, head_dim = queries.shape
    f_at = lax.axis_index("frame")
    r_at = lax.axis_index("row")
    padded = jnp.pad(active, ((1, 1), (1, 1), (0, 0), (0, 0)))
    near = lax.dynamic_slice(
        padded, (f_at * 2, r_at, 0, 0), (4, 3, active.shape[2], active.shape[3])
    )
    bias = ((1 - near).astype(jnp.float32) * NEG).reshape(-1)
    tall = frames_here * rows_here * cols_here * heads_all

    def flat(tensor):
        return jnp.transpose(tensor, (0, 1, 3, 2, 4)).reshape(tall, head_dim)

    def unflat(tensor):
        shaped = tensor.reshape(frames_here, rows_here, heads_all, cols_here, head_dim)
        return jnp.transpose(shaped, (0, 1, 3, 2, 4))

    dma = pltpu.SemaphoreType.DMA
    block = (128, head_dim)
    kinds = heads - 1
    anywhere = pl.BlockSpec(memory_space=pl.ANY)
    results = pl.pallas_call(
        functools.partial(tile_kernel, sizes),
        out_shape=[jax.ShapeDtypeStruct((tall, head_dim), jnp.bfloat16)] * 4,
        in_specs=[pl.BlockSpec(memory_space=pltpu.SMEM)] + [anywhere] * 4,
        out_specs=[anywhere] * 4,
        scratch_shapes=[
            pltpu.VMEM((4, tall, head_dim), jnp.bfloat16),
            pltpu.VMEM((4, heads_all, 2, 32, head_dim), jnp.bfloat16),
            pltpu.VMEM((4, groups, 4, 3) + block, jnp.bfloat16),
            pltpu.VMEM((groups, 4, 3, 8, 128), jnp.float32),
            pltpu.VMEM((4, groups, 2) + block, jnp.bfloat16),
            pltpu.VMEM((4, heads_all, 2, 32, head_dim), jnp.bfloat16),
            dma((4,)),
            dma((4, kinds)),
            dma((4, kinds)),
            dma((5, 2)),
            dma((5, 2)),
            dma((5, 2)),
            dma((5, 2)),
            dma((5, 4)),
            dma((5, 4)),
            dma((4, kinds)),
            dma((4, kinds)),
            dma((4,)),
        ],
        compiler_params=pltpu.CompilerParams(
            collective_id=0, has_side_effects=True, vmem_limit_bytes=48 << 20
        ),
    )(bias, flat(keys), flat(values), flat(queries), flat(out_grad))
    return tuple(unflat(r) for r in results)


def solution(mesh):
    frames, rows, heads = (mesh.shape[a] for a in ("frame", "row", "head"))
    sizes = (frames, rows, heads, 12 // heads, 128**-0.5)
    spec = P("frame", "row", "head", None, None)
    return jax.shard_map(
        functools.partial(on_device, sizes),
        mesh=mesh,
        in_specs=(spec,) * 4 + (P(),),
        out_specs=(spec,) * 4,
        check_vma=False,
    )
```

time: 287 us -> 128 us (0.45)
  Pallas kernels: 0 us -> 122 us
  starting transfers between devices: 114 us -> 0 us
  waiting for transfers between devices: 88.9 us -> 0 us
  local copies, waits for them, and re-layouts: 39.4 us -> 4.97 us
  matrix products: 27.8 us -> 0 us
  other arithmetic: 11.9 us -> 0.03 us
    pallas_call x0 -> x1, Pallas kernels: none -> 122 us  [on_device(): pl.pallas_call(functools.partial(tile_kernel, sizes), out_shape=[jax.Shap...]
    ppermute x12 -> x0, starting transfers between devices: 83.3 us -> none  [the longest x6 73.3 us: padded(): before = lax.ppermute(last, axis, up)]
    ppermute x12 -> x0, waiting for transfers between devices: 72 us -> none  [the longest x6 71.3 us: padded(): after = lax.ppermute(initial, axis, down)]
    all_to_all x8 -> x0, starting transfers between devices: 31.1 us -> none  [the longest x1 4.58 us: on_device(): lax.all_to_all(split_heads(out_grad), 'head', split_axis=3, concat_axis=2...]
    dot_general x38 -> x0, matrix products: 27.8 us -> none  [the longest x18 22.6 us: product(): return jnp.einsum(form, left, right, preferred_element_type=jnp.float32)]
    all_to_all x8 -> x0, waiting for transfers between devices: 16.9 us -> none  [the longest x1 4.56 us: on_device(): lax.all_to_all(split_heads(out_grad), 'head', split_axis=3, concat_axis=2...]
    reshape x8 -> x1, local copies, waits for them, and re-layouts: 8.77 us -> 0.09 us  [on_device(): bias = ((1 - near).astype(jnp.float32) * NEG).reshape(-1)]
    squeeze x12 -> x0, local copies, waits for them, and re-layouts: 7.66 us -> none  [the longest x6 3.3 us: on_device(): lax.map(front, (query_slab, key_wide, value_wide, grad_slab))]
  transfers between devices with their start and end apart: 20 -> 0, of which waited for: 9 -> 0; matrix products, arithmetic and copies ran while one was open for 27% -> 0% of each run, Pallas kernels for 0% -> 0%
where the time goes in v1:
time: 128 us
  Pallas kernels  122 us (95%)
  local copies, waits for them, and re-layouts  4.97 us (4%)
    pallas_call x1, Pallas kernels, on_device(): pl.pallas_call(functools.partial(tile_kernel, sizes), out_shape=[jax.Shap...  122 us
    unnamed x13, local copies, waits for them, and re-layouts  4.87 us

profile of v1, /device:TPU:25, one launch (start us, length us, event | category | flops | bytes accessed | tf_op | source)
XLA Modules:
  0.0 128.1 jit_solution(6914601945871237829)
XLA Ops:
  0.6 0.0 copy-start.2
  0.6 0.0 copy-start.3
  0.7 1.3 %copy.10 = s32[32,16,2,27]{3,0,2,1:T(8,128)S(1)} copy(s32[32,16,2,27]{0,2,3,1:T(2,128)} %param.9) | data formatting | bytes 221184 | tf_op args[4]
  2.0 0.0 copy-start
  2.0 0.0 copy-start.1
  2.1 0.1 reshape.35.bias
  2.2 0.0 copy-done.2
  2.2 0.0 copy-done.3
  2.2 0.7 copy-done
  2.9 0.1 copy-done.1
  3.0 122.3 %shard_map.84 = (bf16[768,128]{1,0:T(8,128)(2,1)S(1)}, bf16[768,128]{1,0:T(8,128)(2,1)S(1)}, bf16[768,128]{1,0:T(8,128)(2,1)S(1)}, bf16[768,128]{1,0:T(8,128)(2,1)S(1)}) custom-call(f32[648]{0:T(1024)S(1)} %reshape.35.bias, bf16[768,128]{1,0:T(8,128)(2,1)S(1)} %bitcast.28, bf16[768,128]{1,0:T(8,128)(2,1)S(1)} %bitcast.29, bf16[768,128]{1,0:T(8,128)(2,1)S(1)} %bitcast.30, ...), custom_call_target="tpu_custom_call" | custom-call | tf_op jit(solution)/shard_map/pallas_call | solution.py:407
  125.3 0.7 copy.16
  126.0 0.7 copy.17
  126.7 0.7 copy.18
  127.4 0.7 copy.19
  (2 shorter events, 0.0 us)
Async XLA Ops:
  0.6 1.5 %copy-start.2 = (bf16[2,8,4,12,128]{4,2,3,1,0:T(4,128)(2,1)S(1)}, bf16[2,8,4,12,128]{4,2,3,1,0:T(4,128)(2,1)}, u32[]{:S(2)}) copy-start(bf16[2,8,4,12,128]{4,2,3,1,0:T(4,128)(2,1)} %param.5) | copy-start | bytes 589828
  0.6 1.5 %copy-start.3 = (bf16[2,8,4,12,128]{4,2,3,1,0:T(4,128)(2,1)S(1)}, bf16[2,8,4,12,128]{4,2,3,1,0:T(4,128)(2,1)}, u32[]{:S(2)}) copy-start(bf16[2,8,4,12,128]{4,2,3,1,0:T(4,128)(2,1)} %param.8) | copy-start | bytes 589828
  2.0 0.9 copy-start
  2.0 1.0 copy-start.1

commit v2 on v1

--- a/solution.py
+++ b/solution.py
@@ -27,9 +27,9 @@
 def tile_kernel(sizes, bias, k_in, v_in, q_in, g_in, *refs):
     frames, rows, heads, groups, scaling = sizes
     outs, refs = refs[:4], refs[4:]
-    land, pack, wide, stats, own, back = refs[:6]
-    in_sem, a_send, a_recv, z_send, z_recv, c_send, c_recv, d_send, d_recv = refs[6:15]
-    o_send, o_recv, out_sem = refs[15:18]
+    land, pack, wide, stats, own, back, relay = refs[:7]
+    in_sem, a_send, a_recv, z_send, z_recv, c_send, c_recv, d_send, d_recv = refs[7:16]
+    o_send, o_recv, out_sem, leg_send, leg_recv = refs[16:21]
     ins = (k_in, v_in, q_in, g_in)
     heads_all = groups * heads
     tall = heads_all * 16
@@ -40,6 +40,31 @@
     up, down = f_at < frames - 1, f_at > 0
     right, left = r_at < rows - 1, r_at > 0
     far_up, far_down = f_at == frames // 2 - 1, f_at == frames // 2
+    both = jnp.logical_and
+    near_up = both(up, jnp.logical_not(far_up))
+    near_down = both(down, jnp.logical_not(far_down))
+    far = jnp.logical_or(far_up, far_down)
+
+    half, turn = frames // 2, 2 * rows
+    upper, place = f_at // half, f_at % half
+    core, column = f_at % 2, place // 2
+    z_at = upper * rows + r_at
+    first_relay = core + upper == 1
+    shifted = lax.rem(z_at + rows * (1 - core), turn)
+    odd = lax.rem(shifted, 2)
+    began = jnp.where(odd == 1, shifted - (rows - 1), lax.rem(shifted + turn - rows - 1, turn))
+    second_relay = both(began >= 0, began < rows) & (lax.rem(began + turn, 2) == 1 - odd)
+
+    def far_spot(z):
+        return lax.rem(z + rows - 1 + 2 * lax.rem(r_at, 2), turn)
+
+    def relays_of(z, member):
+        spot = far_spot(z)
+        return (spot // rows) * half + member, lax.rem(spot, rows)
+
+    def start_relay(t):
+        return upper * half + 2 * t + core, r_at
+
     peers = [lax.rem(x_at + k, heads) for k in range(heads)]
     froms = [lax.rem(x_at + heads - k, heads) for k in range(heads)]
 
@@ -60,6 +85,25 @@
     pl.when(left)(lambda: greet(f_at, r_at - 1, x_at))
     pl.when(up)(lambda: greet(f_at + 1, r_at, x_at))
     pl.when(down)(lambda: greet(f_at - 1, r_at, x_at))
+    origin = (half - 1 + upper, r_at)
+    next_relay = relays_of(z_at, place)
+    last_from = ((1 - core) * half + place, began)
+    last_to = (half - 1 + core, began)
+
+    @pl.when(far)
+    def _():
+        for t in range(4):
+            pl.when(column != t)(lambda: greet(*start_relay(t), x_at))
+            greet(*relays_of(z_at + rows, 2 * t + 1 - core), x_at)
+
+    pl.when(both(first_relay, jnp.logical_not(far)))(lambda: greet(*origin, x_at))
+    pl.when(first_relay)(lambda: greet(*next_relay, x_at))
+
+    @pl.when(second_relay)
+    def _():
+        greet(*last_from, x_at)
+        greet(*last_to, x_at)
+
 
     @pl.when(jnp.logical_not(left))
     def _():
@@ -166,15 +210,46 @@
             block(t, frame, 1), block(t, frame, 2), d_send.at[t, sem], d_recv.at[t, sem], f_at, r_at - 1
         )
 
-    both = jnp.logical_and
-    near_up = both(up, jnp.logical_not(far_up))
-    near_down = both(down, jnp.logical_not(far_down))
+    edge = jnp.where(far_up, 2, 1)
+
+    def leg_one(t):
+        return hop(
+            block(t, edge, 1), relay.at[0], leg_send.at[t], leg_recv.at[0], *start_relay(t)
+        )
+
+    def leg_two(src):
+        return hop(src, relay.at[1], leg_send.at[4], leg_recv.at[1], *next_relay)
+
+    def leg_three(t):
+        side = 1 - core
+        return hop(
+            relay.at[1], block(t, 3 * side, 1), leg_send.at[5], c_recv.at[t, side], *last_to
+        )
 
     def first_halo(t):
-        pl.when(up)(lambda: to_up(t).start())
-        pl.when(down)(lambda: to_down(t).start())
+        out_up, out_down = (up, down) if t == 4 else (near_up, near_down)
+        if t < 4:
+            pl.when(both(far, column != t))(lambda: leg_one(t).start())
         pl.when(right)(lambda: to_right(t).start())
         pl.when(left)(lambda: to_left(t).start())
+        pl.when(out_up)(lambda: to_up(t).start())
+        pl.when(out_down)(lambda: to_down(t).start())
+
+    def relay_one(t):
+        here = both(first_relay, column == t)
+
+        @pl.when(both(here, jnp.logical_not(far)))
+        def _():
+            leg_one(t).wait_recv()
+            leg_two(relay.at[0]).start()
+
+        pl.when(both(here, far))(lambda: leg_two(block(t, edge, 1)).start())
+
+    def relay_two(t):
+        @pl.when(both(second_relay, column == t))
+        def _():
+            leg_two(relay.at[0]).wait_recv()
+            leg_three(t).start()
 
     def second_halo(t):
         pl.when(left)(lambda: to_right(t).wait_recv())
@@ -183,22 +258,53 @@
         pl.when(both(near_up, right))(lambda: side_up(t, 2).start())
         pl.when(both(near_down, left))(lambda: side_down(t, 0).start())
         pl.when(both(near_down, right))(lambda: side_down(t, 2).start())
-        pl.when(down)(lambda: to_up(t).wait_recv())
-        pl.when(up)(lambda: to_down(t).wait_recv())
+
+    def far_halo(t):
+        pl.when(far_down)(lambda: to_up(t).wait_recv())
+        pl.when(far_up)(lambda: to_down(t).wait_recv())
         pl.when(both(far_down, right))(lambda: along_right(t, 0).start())
         pl.when(both(far_down, left))(lambda: along_left(t, 0).start())
         pl.when(both(far_up, right))(lambda: along_right(t, 3).start())
         pl.when(both(far_up, left))(lambda: along_left(t, 3).start())
 
-    def last_halo(t):
+    def low_halo(t):
+        pl.when(near_down)(lambda: to_up(t).wait_recv())
         pl.when(both(down, left))(lambda: side_up(t, 0).wait_recv())
         pl.when(both(down, right))(lambda: side_up(t, 2).wait_recv())
+
+    def high_halo(t):
+        pl.when(near_up)(lambda: to_down(t).wait_recv())
         pl.when(both(up, left))(lambda: side_down(t, 0).wait_recv())
         pl.when(both(up, right))(lambda: side_down(t, 2).wait_recv())
 
+    def early_halo(*kinds):
+        @pl.when(jnp.logical_not(far_down))
+        def _():
+            for t in kinds:
+                low_halo(t)
+
+        @pl.when(far_down)
+        def _():
+            for t in kinds:
+                high_halo(t)
+
+    def late_halo(*kinds):
+        @pl.when(far_down)
+        def _():
+            for t in kinds:
+                low_halo(t)
+
+        @pl.when(jnp.logical_not(far_down))
+        def _():
+            for t in kinds:
+                high_halo(t)
+
     def halo_sent(t):
-        pl.when(up)(lambda: to_up(t).wait_send())
-        pl.when(down)(lambda: to_down(t).wait_send())
+        out_up, out_down = (up, down) if t == 4 else (near_up, near_down)
+        if t < 4:
+            pl.when(both(far, column != t))(lambda: leg_one(t).wait_send())
+        pl.when(out_up)(lambda: to_up(t).wait_send())
+        pl.when(out_down)(lambda: to_down(t).wait_send())
         pl.when(right)(lambda: to_right(t).wait_send())
         pl.when(left)(lambda: to_left(t).wait_send())
         pl.when(both(near_up, left))(lambda: side_up(t, 0).wait_send())
@@ -216,8 +322,10 @@
             part = nn(to_heads, land[t, pl.ds(g * tall, tall)]).astype(jnp.bfloat16)
             pack[t, :, g // 2, pl.ds(16 * (g % 2), 16)] = part.reshape(heads_all, 16, 128)
         if t == 0:
-            known = [right, left, up, down]
-            pl.semaphore_wait(barrier, heads - 1 + sum(c.astype(jnp.int32) for c in known))
+            known = [right, left, up, down, both(first_relay, jnp.logical_not(far)), first_relay]
+            count = heads - 1 + sum(c.astype(jnp.int32) for c in known)
+            count += 2 * second_relay.astype(jnp.int32) + 7 * far.astype(jnp.int32)
+            pl.semaphore_wait(barrier, count)
         for k in range(1, heads):
             exchange(t, k).start()
         wide[t, :, pl.ds(1, 2), 1, pl.ds(pl.multiple_of(x_at * 32, 32), 32)] = pack[
@@ -232,17 +340,23 @@
     first_halo(KEY)
     gathered(VAL)
     first_halo(VAL)
+    relay_one(KEY)
     second_halo(KEY)
     gathered(QRY)
     first_halo(QRY)
+    relay_one(VAL)
     second_halo(VAL)
     gathered(GRD)
     first_halo(GRD)
+    relay_one(QRY)
+    relay_two(KEY)
     second_halo(QRY)
+    relay_one(GRD)
+    relay_two(VAL)
     second_halo(GRD)
-    last_halo(KEY)
-    last_halo(VAL)
-
+    early_halo(KEY, VAL)
+
+    flip = far_down.astype(jnp.int32)
     lanes = lax.broadcasted_iota(jnp.int32, (1, 128), 1)
     lane_grid = lax.broadcasted_iota(jnp.int32, (128, 128), 1)
     power = scaling * math.log2(math.e)
@@ -251,7 +365,7 @@
         return bias[((i * 3 + j) * 2 + l) * SLOTS + slot]
 
     def query_step(i, carry):
-        h, f = i // 2, i % 2
+        h, f = i % groups, (i // groups) ^ flip
         q = wide[QRY, h, f + 1, 1]
         g = wide[GRD, h, f + 1, 1]
         k_band = wide[KEY, h, pl.ds(f, 3)].reshape(9 * 128, 128)
@@ -288,7 +402,13 @@
         stats[h, f + 1, 1] = both_stats.T[0:8]
         return carry
 
-    lax.fori_loop(0, groups * 2, query_step, 0)
+    lax.fori_loop(0, groups, query_step, 0)
+    relay_two(QRY)
+    relay_two(GRD)
+    far_halo(KEY)
+    far_halo(VAL)
+    late_halo(KEY, VAL)
+    lax.fori_loop(groups, groups * 2, query_step, 0)
 
     def giving(o, k):
         spot = pl.ds(pl.multiple_of(peers[k] * 32, 32), 32)
@@ -329,17 +449,15 @@
         storing(o).start()
 
     first_halo(4)
+    far_halo(QRY)
+    far_halo(GRD)
     give(0)
     give(1)
     second_halo(4)
-    last_halo(QRY)
-    last_halo(GRD)
-    finish(0)
-    finish(1)
-    last_halo(4)
+    early_halo(QRY, GRD, 4)
 
     def key_step(i, carry):
-        h, f = i // 2, i % 2
+        h, f = i % groups, (i // groups) ^ flip
         k = wide[KEY, h, f + 1, 1]
         v = wide[VAL, h, f + 1, 1]
         q_band = wide[QRY, h, pl.ds(f, 3)].reshape(9 * 128, 128)
@@ -365,9 +483,14 @@
         own[2, h, f] = (nn(ds, q_band) * scaling).astype(jnp.bfloat16)
         return carry
 
-    lax.fori_loop(0, groups * 2, key_step, 0)
+    lax.fori_loop(0, groups, key_step, 0)
+    far_halo(4)
+    late_halo(QRY, GRD, 4)
+    lax.fori_loop(groups, groups * 2, key_step, 0)
     give(2)
     give(3)
+    finish(0)
+    finish(1)
     finish(2)
     finish(3)
 
@@ -377,6 +500,8 @@
             giving(t, k).wait_send()
     for t in range(5):
         halo_sent(t)
+    pl.when(first_relay)(lambda: leg_two(relay.at[0]).wait_send())
+    pl.when(second_relay)(lambda: leg_three(0).wait_send())
     for o in range(4):
         storing(o).wait()
 
@@ -416,6 +541,7 @@
             pltpu.VMEM((groups, 4, 3, 8, 128), jnp.float32),
             pltpu.VMEM((4, groups, 2) + block, jnp.bfloat16),
             pltpu.VMEM((4, heads_all, 2, 32, head_dim), jnp.bfloat16),
+            pltpu.VMEM((2, groups) + block, jnp.bfloat16),
             dma((4,)),
             dma((4, kinds)),
             dma((4, kinds)),
@@ -428,6 +554,8 @@
             dma((4, kinds)),
             dma((4, kinds)),
             dma((4,)),
+            dma((6,)),
+            dma((2,)),
         ],
         compiler_params=pltpu.CompilerParams(
             collective_id=0, has_side_effects=True, vmem_limit_bytes=48 << 20

time: 128 us -> 99.6 us (0.78)
  Pallas kernels: 122 us -> 93.7 us
    pallas_call x1, Pallas kernels: 122 us -> 93.7 us  [on_device(): pl.pallas_call(functools.partial(tile_kernel, sizes), out_shape=[jax.Shap...]
where the time goes in v2:
time: 99.6 us; the launch traced here: 99.4 us
  Pallas kernels  93.7 us (94%)
  local copies, waits for them, and re-layouts  4.97 us (5%)
    pallas_call x1, Pallas kernels, on_device(): pl.pallas_call(functools.partial(tile_kernel, sizes), out_shape=[jax.Shap...  93.7 us
    unnamed x13, local copies, waits for them, and re-layouts  4.87 us

profile of v2, /device:TPU:25, one launch (start us, length us, event | category | flops | bytes accessed | tf_op | source)
XLA Modules:
  0.0 99.4 jit_solution(16964207473044655871)
XLA Ops:
  0.6 0.0 copy-start.2
  0.6 0.0 copy-start.3
  0.7 1.3 %copy.10 = s32[32,16,2,27]{3,0,2,1:T(8,128)S(1)} copy(s32[32,16,2,27]{0,2,3,1:T(2,128)} %param.9) | data formatting | bytes 221184 | tf_op args[4]
  2.0 0.0 copy-start
  2.0 0.0 copy-start.1
  2.1 0.1 reshape.35.bias
  2.2 0.0 copy-done.2
  2.2 0.0 copy-done.3
  2.2 0.7 copy-done
  2.9 0.1 copy-done.1
  3.0 93.7 %shard_map.84 = (bf16[768,128]{1,0:T(8,128)(2,1)S(1)}, bf16[768,128]{1,0:T(8,128)(2,1)S(1)}, bf16[768,128]{1,0:T(8,128)(2,1)S(1)}, bf16[768,128]{1,0:T(8,128)(2,1)S(1)}) custom-call(f32[648]{0:T(1024)S(1)} %reshape.35.bias, bf16[768,128]{1,0:T(8,128)(2,1)S(1)} %bitcast.28, bf16[768,128]{1,0:T(8,128)(2,1)S(1)} %bitcast.29, bf16[768,128]{1,0:T(8,128)(2,1)S(1)} %bitcast.30, ...), custom_call_target="tpu_custom_call" | custom-call | tf_op jit(solution)/shard_map/pallas_call | solution.py:532
  96.7 0.7 copy.16
  97.4 0.7 copy.17
  98.1 0.7 copy.18
  98.7 0.7 copy.19
  (2 shorter events, 0.0 us)
Async XLA Ops:
  0.6 1.5 %copy-start.2 = (bf16[2,8,4,12,128]{4,2,3,1,0:T(4,128)(2,1)S(1)}, bf16[2,8,4,12,128]{4,2,3,1,0:T(4,128)(2,1)}, u32[]{:S(2)}) copy-start(bf16[2,8,4,12,128]{4,2,3,1,0:T(4,128)(2,1)} %param.5) | copy-start | bytes 589828
  0.6 1.5 %copy-start.3 = (bf16[2,8,4,12,128]{4,2,3,1,0:T(4,128)(2,1)S(1)}, bf16[2,8,4,12,128]{4,2,3,1,0:T(4,128)(2,1)}, u32[]{:S(2)}) copy-start(bf16[2,8,4,12,128]{4,2,3,1,0:T(4,128)(2,1)} %param.8) | copy-start | bytes 589828
  2.0 0.9 copy-start
  2.0 1.0 %copy-start.1 = (bf16[2,8,4,12,128]{4,2,3,1,0:T(4,128)(2,1)S(1)}, bf16[2,8,4,12,128]{4,2,3,1,0:T(4,128)(2,1)}, u32[]{:S(2)}) copy-start(bf16[2,8,4,12,128]{4,2,3,1,0:T(4,128)(2,1)} %param.7) | copy-start | bytes 589828

commit v3 on v1

v3 whole, which is shorter than its diff:
```python
import functools
import math

import jax
import jax.numpy as jnp
from jax import lax
from jax.experimental import pallas as pl
from jax.experimental.pallas import tpu as pltpu
from jax.sharding import PartitionSpec as P

MESH = pl.DeviceIdType.MESH
NEG = -1e30
KEY, VAL, QRY, GRD = 0, 1, 2, 3
SLOTS = 27


def nt(left, right):
    return lax.dot_general(
        left, right, (((1,), (1,)), ((), ())), preferred_element_type=jnp.float32
    )


def nn(left, right):
    return jnp.dot(left, right, preferred_element_type=jnp.float32)


def tile_kernel(sizes, act_in, k_in, v_in, q_in, g_in, *refs):
    frames, rows, heads, groups, scaling = sizes
    outs, refs = refs[:4], refs[4:]
    land, pack, wide, stats, own, back, part, front, behind, across, act = refs[:11]
    in_sem, a_send, a_recv, z_send, z_recv, c_send, c_recv, d_send, d_recv = refs[11:20]
    o_send, o_recv, out_sem, part_sem, act_sem, ready = refs[20:26]
    ins = (k_in, v_in, q_in, g_in)
    heads_all = groups * heads
    tall = heads_all * 16

    f_at = lax.axis_index("frame")
    r_at = lax.axis_index("row")
    x_at = lax.axis_index("head")
    up, down = f_at < frames - 1, f_at > 0
    right, left = r_at < rows - 1, r_at > 0
    far_up, far_down = f_at == frames // 2 - 1, f_at == frames // 2
    both = jnp.logical_and
    near_up = both(up, jnp.logical_not(far_up))
    near_down = both(down, jnp.logical_not(far_down))
    far = jnp.logical_or(far_up, far_down)

    half = frames // 2
    spread = min(3, half - 1)
    proxy_up, proxy_down = f_at == half - 1 - spread, f_at == half + spread
    proxy = jnp.logical_or(proxy_up, proxy_down)
    edge = far_up.astype(jnp.int32)
    beyond = 3 * edge
    flip = far_down.astype(jnp.int32)

    peers = [lax.rem(x_at + k, heads) for k in range(heads)]
    froms = [lax.rem(x_at + heads - k, heads) for k in range(heads)]

    def loading(t):
        return pltpu.make_async_copy(ins[t], land.at[t], in_sem.at[t])

    def loading_act(j):
        row = jnp.clip(r_at - 1 + j, 0, rows - 1)
        return pltpu.make_async_copy(act_in.at[row], act.at[j], act_sem.at[j])

    for t in range(4):
        loading(t).start()
    for j in range(3):
        loading_act(j).start()

    barrier = pltpu.get_barrier_semaphore()

    def greet(frame, row, head):
        pl.semaphore_signal(barrier, inc=1, device_id=(frame, row, head), device_id_type=MESH)

    for k in range(1, heads):
        greet(f_at, r_at, peers[k])
    pl.when(right)(lambda: greet(f_at, r_at + 1, x_at))
    pl.when(left)(lambda: greet(f_at, r_at - 1, x_at))
    pl.when(near_up)(lambda: greet(f_at + 1, r_at, x_at))
    pl.when(near_down)(lambda: greet(f_at - 1, r_at, x_at))

    @pl.when(far)
    def _():
        greet(jnp.where(far_up, half - 1 - spread, half + spread), r_at, x_at)
        greet(jnp.where(far_up, half + spread, half - 1 - spread), r_at, x_at)

    @pl.when(jnp.logical_not(left))
    def _():
        wide[:, :, :, 0] = jnp.zeros_like(wide[:, :, :, 0])
        stats[:, :, 0] = jnp.zeros_like(stats[:, :, 0])

    @pl.when(jnp.logical_not(right))
    def _():
        wide[:, :, :, 2] = jnp.zeros_like(wide[:, :, :, 2])
        stats[:, :, 2] = jnp.zeros_like(stats[:, :, 2])

    @pl.when(jnp.logical_not(down))
    def _():
        wide[:, :, 0] = jnp.zeros_like(wide[:, :, 0])
        stats[:, 0] = jnp.zeros_like(stats[:, 0])

    @pl.when(jnp.logical_not(up))
    def _():
        wide[:, :, 3] = jnp.zeros_like(wide[:, :, 3])
        stats[:, 3] = jnp.zeros_like(stats[:, 3])

    out_row = lax.broadcasted_iota(jnp.int32, (tall, tall), 0)
    in_row = lax.broadcasted_iota(jnp.int32, (tall, tall), 1)

    def swapped(row):
        return ((row % 16) // 4) * (4 * heads_all) + (row // 16) * 4 + row % 4

    to_heads = (swapped(out_row) == in_row).astype(jnp.bfloat16)
    to_rows = (swapped(in_row) == out_row).astype(jnp.bfloat16)

    def exchange(t, k):
        there = peers[k]
        return pltpu.make_async_remote_copy(
            src_ref=pack.at[t, pl.ds(there * groups, groups)],
            dst_ref=wide.at[t, :, pl.ds(1, 2), 1, pl.ds(pl.multiple_of(x_at * 32, 32), 32)],
            send_sem=a_send.at[t, k - 1],
            recv_sem=a_recv.at[t, k - 1],
            device_id=(f_at, r_at, there),
            device_id_type=MESH,
        )

    def arriving(t, k):
        spot = pl.ds(pl.multiple_of(froms[k] * 32, 32), 32)
        return pltpu.make_async_remote_copy(
            src_ref=pack.at[t, pl.ds(0, groups)],
            dst_ref=wide.at[t, :, pl.ds(1, 2), 1, spot],
            send_sem=a_send.at[t, k - 1],
            recv_sem=a_recv.at[t, k - 1],
            device_id=(f_at, r_at, froms[k]),
            device_id_type=MESH,
        )

    def block(t, frame, row):
        ref = stats if t == 4 else wide.at[t]
        return ref.at[:, frame, row]

    def pair(t, row):
        ref = stats if t == 4 else wide.at[t]
        return ref.at[:, pl.ds(1, 2), row]

    def hop(src, dst, ss, rs, frame, row):
        return pltpu.make_async_remote_copy(
            src_ref=src,
            dst_ref=dst,
            send_sem=ss,
            recv_sem=rs,
            device_id=(frame, row, x_at),
            device_id_type=MESH,
        )

    def to_right(t):
        return hop(pair(t, 1), pair(t, 0), z_send.at[t, 0], z_recv.at[t, 0], f_at, r_at + 1)

    def to_left(t):
        return hop(pair(t, 1), pair(t, 2), z_send.at[t, 1], z_recv.at[t, 1], f_at, r_at - 1)

    def to_up(t):
        return hop(block(t, 2, 1), block(t, 0, 1), c_send.at[t, 0], c_recv.at[t, 0], f_at + 1, r_at)

    def to_down(t):
        return hop(block(t, 1, 1), block(t, 3, 1), c_send.at[t, 1], c_recv.at[t, 1], f_at - 1, r_at)

    def side_up(t, row):
        sem = 0 if row == 0 else 1
        return hop(
            block(t, 2, row), block(t, 0, row), d_send.at[t, sem], d_recv.at[t, sem], f_at + 1, r_at
        )

    def side_down(t, row):
        sem = 2 if row == 0 else 3
        return hop(
            block(t, 1, row), block(t, 3, row), d_send.at[t, sem], d_recv.at[t, sem], f_at - 1, r_at
        )

    def along_right(t, frame):
        sem = 0 if frame == 0 else 2
        return hop(
            block(t, frame, 1), block(t, frame, 0), d_send.at[t, sem], d_recv.at[t, sem], f_at, r_at + 1
        )

    def along_left(t, frame):
        sem = 1 if frame == 0 else 3
        return hop(
            block(t, frame, 1), block(t, frame, 2), d_send.at[t, sem], d_recv.at[t, sem], f_at, r_at - 1
        )

    def tell():
        pair_at = jnp.where(proxy_up, half - 1, half)
        pl.semaphore_signal(ready, inc=1, device_id=(pair_at, r_at, x_at), device_id_type=MESH)

    def first_halo(t):
        pl.when(right)(lambda: to_right(t).start())
        pl.when(left)(lambda: to_left(t).start())
        pl.when(near_up)(lambda: to_up(t).start())
        pl.when(near_down)(lambda: to_down(t).start())

    def summary(side):
        there = jnp.where(far_up, half, half - 1)
        return hop(part.at[0], part.at[1], part_sem.at[0], part_sem.at[1], there, r_at)

    def second_halo(t):
        pl.when(left)(lambda: to_right(t).wait_recv())
        pl.when(right)(lambda: to_left(t).wait_recv())
        pl.when(both(near_up, left))(lambda: side_up(t, 0).start())
        pl.when(both(near_up, right))(lambda: side_up(t, 2).start())
        pl.when(both(near_down, left))(lambda: side_down(t, 0).start())
        pl.when(both(near_down, right))(lambda: side_down(t, 2).start())

    def far_halo(t):
        if t < 4:
            pl.when(far_down)(lambda: to_up(t).wait_recv())
            pl.when(far_up)(lambda: to_down(t).wait_recv())
        pl.when(both(far_down, right))(lambda: along_right(t, 0).start())
        pl.when(both(far_down, left))(lambda: along_left(t, 0).start())
        pl.when(both(far_up, right))(lambda: along_right(t, 3).start())
        pl.when(both(far_up, left))(lambda: along_left(t, 3).start())

    def low_halo(t):
        pl.when(near_down)(lambda: to_up(t).wait_recv())
        pl.when(both(down, left))(lambda: side_up(t, 0).wait_recv())
        pl.when(both(down, right))(lambda: side_up(t, 2).wait_recv())

    def high_halo(t):
        pl.when(near_up)(lambda: to_down(t).wait_recv())
        pl.when(both(up, left))(lambda: side_down(t, 0).wait_recv())
        pl.when(both(up, right))(lambda: side_down(t, 2).wait_recv())

    def early_halo(*kinds):
        @pl.when(jnp.logical_not(far_down))
        def _():
            for t in kinds:
                low_halo(t)

        @pl.when(far_down)
        def _():
            for t in kinds:
                high_halo(t)

    def late_halo(*kinds):
        @pl.when(far_down)
        def _():
            for t in kinds:
                low_halo(t)

        @pl.when(jnp.logical_not(far_down))
        def _():
            for t in kinds:
                high_halo(t)

    def halo_sent(t):
        out_up, out_down = (up, down) if t < 4 else (near_up, near_down)
        pl.when(out_up)(lambda: to_up(t).wait_send())
        pl.when(out_down)(lambda: to_down(t).wait_send())
        pl.when(right)(lambda: to_right(t).wait_send())
        pl.when(left)(lambda: to_left(t).wait_send())
        pl.when(both(near_up, left))(lambda: side_up(t, 0).wait_send())
        pl.when(both(near_up, right))(lambda: side_up(t, 2).wait_send())
        pl.when(both(near_down, left))(lambda: side_down(t, 0).wait_send())
        pl.when(both(near_down, right))(lambda: side_down(t, 2).wait_send())
        pl.when(both(far_down, right))(lambda: along_right(t, 0).wait_send())
        pl.when(both(far_down, left))(lambda: along_left(t, 0).wait_send())
        pl.when(both(far_up, right))(lambda: along_right(t, 3).wait_send())
        pl.when(both(far_up, left))(lambda: along_left(t, 3).wait_send())

    for j in range(3):
        loading_act(j).wait()

    lanes = lax.broadcasted_iota(jnp.int32, (1, 128), 1)

    def placed(i, j):
        frame, row = 2 * f_at - 1 + i, r_at - 1 + j
        return (frame >= 0) & (frame < 2 * frames) & (row >= 0) & (row < rows)

    def entry(i, j, l, slot, inside):
        frame = jnp.clip(2 * f_at - 1 + i, 0, 2 * frames - 1)
        return jnp.where(inside & (act[j, slot, l, frame] == 1), 0.0, NEG)

    def halves(pair_of):
        return jnp.where(lanes < 64, pair_of[0], pair_of[1])

    def mask_step(i, carry):
        f, a = i // 3, i % 3
        for b in range(3):
            span = pl.ds(pl.multiple_of(a * 384 + b * 128, 128), 128)
            inside = placed(f + a, b)
            for l in range(2):
                slots = [9 * a + 3 * b + m - l + 1 for m in range(2)]
                front[f, l, :, span] = halves([entry(f + 1, 1, l, n, inside) for n in slots])
                slots = [9 * (2 - a) + 3 * (2 - b) + l - m + 1 for m in range(2)]
                behind[f, l, :, span] = halves([entry(f + a, b, l, n, inside) for n in slots])
        return carry

    lax.fori_loop(0, 6, mask_step, 0)

    @pl.when(far)
    def _():
        for b in range(3):
            inside = placed(edge + 1, b)
            for l in range(2):
                slots = [18 * (1 - edge) + 3 * b + l - m + 1 for m in range(2)]
                pieces = [entry(beyond, 1, m, n, inside) for m, n in enumerate(slots)]
                across[2 * b + l] = halves(pieces)

    for t in range(4):
        loading(t).wait()
        for g in range(4):
            moved = nn(to_heads, land[t, pl.ds(g * tall, tall)]).astype(jnp.bfloat16)
            pack[t, :, g // 2, pl.ds(16 * (g % 2), 16)] = moved.reshape(heads_all, 16, 128)
        if t == 0:
            known = [right, left, near_up, near_down, proxy, proxy]
            pl.semaphore_wait(barrier, heads - 1 + sum(c.astype(jnp.int32) for c in known))
            pl.when(proxy)(tell)
        for k in range(1, heads):
            exchange(t, k).start()
        wide[t, :, pl.ds(1, 2), 1, pl.ds(pl.multiple_of(x_at * 32, 32), 32)] = pack[
            t, pl.ds(x_at * groups, groups)
        ]

    def gathered(t):
        for k in range(1, heads):
            arriving(t, k).wait_recv()

    gathered(KEY)
    first_halo(KEY)
    gathered(VAL)
    first_halo(VAL)
    second_halo(KEY)
    gathered(QRY)
    first_halo(QRY)
    second_halo(VAL)
    gathered(GRD)
    first_halo(GRD)

    @pl.when(far)
    def _():
        pl.semaphore_wait(ready, 1)
        for t in range(4):
            pl.when(far_up)(lambda: to_up(t).start())
            pl.when(far_down)(lambda: to_down(t).start())

    second_halo(QRY)
    second_halo(GRD)

    lane_grid = lax.broadcasted_iota(jnp.int32, (128, 128), 1)
    power = scaling * math.log2(math.e)
    wide_rows = 9 * 128

    def as_rows(level, dot):
        return jnp.where(lane_grid == 0, level, dot).T[0:8]

    def query_step(i, carry):
        h, f = i % groups, (i // groups) ^ flip
        q = wide[QRY, h, f + 1, 1]
        g = wide[GRD, h, f + 1, 1]
        k_band = wide[KEY, h, pl.ds(f, 3)].reshape(wide_rows, 128)
        v_band = wide[VAL, h, pl.ds(f, 3)].reshape(wide_rows, 128)
        s = (nt(q, k_band).reshape(2, 64, wide_rows) + front[f]).reshape(128, wide_rows)
        top = jnp.max(s, axis=1, keepdims=True)
        p = jnp.exp2((s - top) * power)
        total = jnp.sum(p, axis=1, keepdims=True)
        inverse = 1.0 / total
        out = (nn(p.astype(jnp.bfloat16), v_band) * inverse).astype(jnp.bfloat16)
        own[0, h, f] = out
        dot = jnp.sum(g.astype(jnp.float32) * out.astype(jnp.float32), axis=1, keepdims=True)
        ds = (p * (nt(g, v_band) - dot)).astype(jnp.bfloat16)
        own[1, h, f] = (nn(ds, k_band) * (inverse * scaling)).astype(jnp.bfloat16)
        stats[h, f + 1, 1] = as_rows(top * power + jnp.log2(total), dot)
        return carry

    def near_step(h, carry):
        q = wide[QRY, h, edge + 1, 1]
        g = wide[GRD, h, edge + 1, 1]
        k_band = wide[KEY, h, pl.ds(1, 2)].reshape(6 * 128, 128)
        v_band = wide[VAL, h, pl.ds(1, 2)].reshape(6 * 128, 128)
        offset = pl.multiple_of((1 - edge) * 384, 128)
        mask = front[edge, :, :, pl.ds(offset, 768)]
        s = (nt(q, k_band).reshape(2, 64, 768) + mask).reshape(128, 768)
        top = jnp.max(s, axis=1, keepdims=True)
        p = jnp.exp2((s - top) * power)
        total = jnp.sum(p, axis=1, keepdims=True)
        dot = jnp.sum(p * nt(g, v_band), axis=1, keepdims=True) / total
        part[0, h] = as_rows(top * power + jnp.log2(total), dot)
        return carry

    def across_step(h, carry):
        q = wide[QRY, h, beyond, 1]
        g = wide[GRD, h, beyond, 1]
        k_band = wide[KEY, h, edge + 1].reshape(384, 128)
        v_band = wide[VAL, h, edge + 1].reshape(384, 128)
        s = ((nt(k_band, q) * power).reshape(6, 64, 128) + across[...]).reshape(384, 128)
        top = jnp.max(s, axis=0, keepdims=True)
        p = jnp.exp2(s - top)
        total = jnp.sum(p, axis=0, keepdims=True)
        dot = jnp.sum(p * nt(v_band, g), axis=0, keepdims=True) / total
        level = top + jnp.log2(total)
        level_near, dot_near = part[1, h, 0:1], part[1, h, 1:2]
        peak = jnp.maximum(level, level_near)
        whole = peak + jnp.log2(jnp.exp2(level - peak) + jnp.exp2(level_near - peak))
        mixed = jnp.exp2(level - whole) * dot + jnp.exp2(level_near - whole) * dot_near
        stats[h, beyond, 1, 0:1] = whole
        stats[h, beyond, 1, 1:2] = mixed
        return carry

    def key_step(i, carry):
        h, f = i % groups, (i // groups) ^ flip
        k = wide[KEY, h, f + 1, 1]
        v = wide[VAL, h, f + 1, 1]
        q_band = wide[QRY, h, pl.ds(f, 3)].reshape(wide_rows, 128)
        g_band = wide[GRD, h, pl.ds(f, 3)].reshape(wide_rows, 128)
        tiles = [stats[h, f + a, b] for a in range(3) for b in range(3)]
        level = jnp.concatenate([t[0:1] for t in tiles], axis=1)
        dot = jnp.concatenate([t[1:2] for t in tiles], axis=1)
        s = (nt(k, q_band) * power).reshape(2, 64, wide_rows) + (behind[f] - level)
        p = jnp.exp2(s.reshape(128, wide_rows))
        own[3, h, f] = nn(p.astype(jnp.bfloat16), g_band).astype(jnp.bfloat16)
        ds = (p * (nt(v, g_band) - dot)).astype(jnp.bfloat16)
        own[2, h, f] = (nn(ds, q_band) * scaling).astype(jnp.bfloat16)
        return carry

    def giving(o, half_at, k):
        f = half_at ^ flip
        spot = pl.ds(pl.multiple_of(peers[k] * 32, 32), 32)
        return pltpu.make_async_remote_copy(
            src_ref=own.at[o, :, f, spot],
            dst_ref=back.at[o, pl.ds(x_at * groups, groups), f],
            send_sem=o_send.at[o, half_at, k - 1],
            recv_sem=o_recv.at[o, half_at, k - 1],
            device_id=(f_at, r_at, peers[k]),
            device_id_type=MESH,
        )

    def taking(o, half_at, k):
        f = half_at ^ flip
        return pltpu.make_async_remote_copy(
            src_ref=own.at[o, :, f, pl.ds(0, 32)],
            dst_ref=back.at[o, pl.ds(froms[k] * groups, groups), f],
            send_sem=o_send.at[o, half_at, k - 1],
            recv_sem=o_recv.at[o, half_at, k - 1],
            device_id=(f_at, r_at, froms[k]),
            device_id_type=MESH,
        )

    def give(half_at, *kinds):
        f = half_at ^ flip
        for o in kinds:
            for k in range(1, heads):
                giving(o, half_at, k).start()
        for o in kinds:
            spot = pl.ds(pl.multiple_of(x_at * 32, 32), 32)
            back[o, pl.ds(x_at * groups, groups), f] = own[o, :, f, spot]

    def storing(o, half_at):
        f = half_at ^ flip
        span = pl.ds(pl.multiple_of(f * 2 * tall, 2 * tall), 2 * tall)
        return pltpu.make_async_copy(land.at[o, span], outs[o].at[span], out_sem.at[o, half_at])

    def finish(half_at, *kinds):
        f = half_at ^ flip
        for o in kinds:
            for k in range(1, heads):
                taking(o, half_at, k).wait_recv()
            for g in range(2):
                piece = back[o, :, f, pl.ds(16 * g, 16)].reshape(tall, 128)
                span = pl.ds(pl.multiple_of((f * 2 + g) * tall, tall), tall)
                land[o, span] = nn(to_rows, piece).astype(jnp.bfloat16)
            storing(o, half_at).start()

    early_halo(KEY, VAL)
    lax.fori_loop(0, groups, query_step, 0)
    give(0, 0, 1)

    @pl.when(far)
    def _():
        lax.fori_loop(0, groups, near_step, 0)
        summary(0).start()

    for t in range(4):
        far_halo(t)

    @pl.when(far)
    def _():
        summary(0).wait_recv()
        lax.fori_loop(0, groups, across_step, 0)

    far_halo(4)
    late_halo(KEY, VAL)
    lax.fori_loop(groups, groups * 2, query_step, 0)
    first_halo(4)
    give(1, 0, 1)
    finish(0, 0, 1)
    second_halo(4)
    early_halo(QRY, GRD, 4)
    lax.fori_loop(0, groups, key_step, 0)
    give(0, 2, 3)
    finish(1, 0, 1)
    late_halo(QRY, GRD, 4)
    lax.fori_loop(groups, groups * 2, key_step, 0)
    give(1, 2, 3)
    finish(0, 2, 3)
    finish(1, 2, 3)

    for t in range(4):
        for k in range(1, heads):
            exchange(t, k).wait_send()
            giving(t, 0, k).wait_send()
            giving(t, 1, k).wait_send()
    for t in range(5):
        halo_sent(t)
    pl.when(far)(lambda: summary(0).wait_send())
    for o in range(4):
        storing(o, 0).wait()
        storing(o, 1).wait()


def on_device(sizes, queries, keys, values, out_grad, active):
    frames, rows, heads, groups, scaling = sizes
    frames_here, rows_here, cols_here, heads_all, head_dim = queries.shape
    table = jnp.transpose(active, (1, 3, 2, 0))
    tall = frames_here * rows_here * cols_here * heads_all

    def flat(tensor):
        return jnp.transpose(tensor, (0, 1, 3, 2, 4)).reshape(tall, head_dim)

    def unflat(tensor):
        shaped = tensor.reshape(frames_here, rows_here, heads_all, cols_here, head_dim)
        return jnp.transpose(shaped, (0, 1, 3, 2, 4))

    dma = pltpu.SemaphoreType.DMA
    block = (128, head_dim)
    kinds = heads - 1
    anywhere = pl.BlockSpec(memory_space=pl.ANY)
    results = pl.pallas_call(
        functools.partial(tile_kernel, sizes),
        out_shape=[jax.ShapeDtypeStruct((tall, head_dim), jnp.bfloat16)] * 4,
        in_specs=[anywhere] * 5,
        out_specs=[anywhere] * 4,
        scratch_shapes=[
            pltpu.VMEM((4, tall, head_dim), jnp.bfloat16),
            pltpu.VMEM((4, heads_all, 2, 32, head_dim), jnp.bfloat16),
            pltpu.VMEM((4, groups, 4, 3) + block, jnp.bfloat16),
            pltpu.VMEM((groups, 4, 3, 8, 128), jnp.float32),
            pltpu.VMEM((4, groups, 2) + block, jnp.bfloat16),
            pltpu.VMEM((4, heads_all, 2, 32, head_dim), jnp.bfloat16),
            pltpu.VMEM((2, groups, 8, 128), jnp.float32),
            pltpu.VMEM((2, 2, 1, 9 * 128), jnp.float32),
            pltpu.VMEM((2, 2, 1, 9 * 128), jnp.float32),
            pltpu.VMEM((6, 1, 128), jnp.float32),
            pltpu.SMEM((3,) + table.shape[1:], jnp.int32),
            dma((4,)),
            dma((4, kinds)),
            dma((4, kinds)),
            dma((5, 2)),
            dma((5, 2)),
            dma((5, 2)),
            dma((5, 2)),
            dma((5, 4)),
            dma((5, 4)),
            dma((4, 2, kinds)),
            dma((4, 2, kinds)),
            dma((4, 2)),
            dma((2,)),
            dma((3,)),
            pltpu.SemaphoreType.REGULAR,
        ],
        compiler_params=pltpu.CompilerParams(
            collective_id=0, has_side_effects=True, vmem_limit_bytes=48 << 20
        ),
    )(table, flat(keys), flat(values), flat(queries), flat(out_grad))
    return tuple(unflat(r) for r in results)


def solution(mesh):
    frames, rows, heads = (mesh.shape[a] for a in ("frame", "row", "head"))
    sizes = (frames, rows, heads, 12 // heads, 128**-0.5)
    spec = P("frame", "row", "head", None, None)
    return jax.shard_map(
        functools.partial(on_device, sizes),
        mesh=mesh,
        in_specs=(spec,) * 4 + (P(),),
        out_specs=(spec,) * 4,
        check_vma=False,
    )
```

time: 128 us -> 112 us (0.88)
  Pallas kernels: 122 us -> 104 us
  local copies, waits for them, and re-layouts: 4.97 us -> 7.42 us
    pallas_call x1, Pallas kernels: 122 us -> 104 us  [on_device(): pl.pallas_call(functools.partial(tile_kernel, sizes), out_shape=[jax.Shap...]
    unnamed x13 -> x14, local copies, waits for them, and re-layouts: 4.87 us -> 7.42 us
where the time goes in v3:
time: 112 us
  Pallas kernels  104 us (93%)
  local copies, waits for them, and re-layouts  7.42 us (7%)
    pallas_call x1, Pallas kernels, on_device(): pl.pallas_call(functools.partial(tile_kernel, sizes), out_shape=[jax.Shap...  104 us
    unnamed x14, local copies, waits for them, and re-layouts  7.42 us

profile of v3, /device:TPU:25, one launch (start us, length us, event | category | flops | bytes accessed | tf_op | source)
XLA Modules:
  0.0 112.1 jit_solution(3340080692183307540)
XLA Ops:
  0.6 0.0 copy-start
  0.6 1.0 copy-done
  1.6 0.0 copy-start.1
  1.6 0.9 copy-done.1
  2.6 0.0 copy-start.2
  2.6 0.9 copy-done.2
  3.5 0.0 copy-start.3
  3.5 0.9 copy-done.3
  4.4 0.0 copy-start.4
  4.4 0.9 copy-done.4
  5.4 104.0 %shard_map.84 = (bf16[768,128]{1,0:T(8,128)(2,1)S(1)}, bf16[768,128]{1,0:T(8,128)(2,1)S(1)}, bf16[768,128]{1,0:T(8,128)(2,1)S(1)}, bf16[768,128]{1,0:T(8,128)(2,1)S(1)}) custom-call(s32[16,27,2,32]{3,2,1,0:T(2,128)S(1)} %bitcast.25, bf16[768,128]{1,0:T(8,128)(2,1)S(1)} %bitcast.26, bf16[768,128]{1,0:T(8,128)(2,1)S(1)} %bitcast.27, ...), custom_call_target="tpu_custom_call" | custom-call | tf_op jit(solution)/shard_map/pallas_call | solution.py:538
  109.4 0.7 copy.13
  110.1 0.7 copy.14
  110.8 0.7 copy.15
  111.4 0.7 copy.16
Async XLA Ops:
  0.6 1.0 copy-start
  1.6 0.9 copy-start.1
  2.6 0.9 copy-start.2
  3.5 0.9 copy-start.3
  4.4 0.9 copy-start.4

commit v4 on v3

--- a/solution.py
+++ b/solution.py
@@ -11,7 +11,7 @@
 MESH = pl.DeviceIdType.MESH
 NEG = -1e30
 KEY, VAL, QRY, GRD = 0, 1, 2, 3
-SLOTS = 27
+VMEM = 63 << 20
 
 
 def nt(left, right):
@@ -27,9 +27,9 @@
 def tile_kernel(sizes, act_in, k_in, v_in, q_in, g_in, *refs):
     frames, rows, heads, groups, scaling = sizes
     outs, refs = refs[:4], refs[4:]
-    land, pack, wide, stats, own, back, part, front, behind, across, act = refs[:11]
-    in_sem, a_send, a_recv, z_send, z_recv, c_send, c_recv, d_send, d_recv = refs[11:20]
-    o_send, o_recv, out_sem, part_sem, act_sem, ready = refs[20:26]
+    land, pack, wide, stats, own, back, part, front, behind, across, relay, act = refs[:12]
+    in_sem, a_send, a_recv, z_send, z_recv, c_send, c_recv, d_send, d_recv = refs[12:21]
+    o_send, o_recv, out_sem, part_sem, act_sem, leg_send, leg_recv, ready = refs[21:29]
     ins = (k_in, v_in, q_in, g_in)
     heads_all = groups * heads
     tall = heads_all * 16
@@ -45,10 +45,30 @@
     near_down = both(down, jnp.logical_not(far_down))
     far = jnp.logical_or(far_up, far_down)
 
-    half = frames // 2
-    spread = min(3, half - 1)
-    proxy_up, proxy_down = f_at == half - 1 - spread, f_at == half + spread
-    proxy = jnp.logical_or(proxy_up, proxy_down)
+    half, turn = frames // 2, 2 * rows
+    upper, place = f_at // half, f_at % half
+    core, column = f_at % 2, place // 2
+    z_at = upper * rows + r_at
+    first_relay = core + upper == 1
+    shifted = lax.rem(z_at + rows * (1 - core), turn)
+    odd = lax.rem(shifted, 2)
+    began = jnp.where(odd == 1, shifted - (rows - 1), lax.rem(shifted + turn - rows - 1, turn))
+    second_relay = both(began >= 0, began < rows) & (lax.rem(began + turn, 2) == 1 - odd)
+    near = jnp.logical_not(far)
+
+    def relays_of(z, member):
+        spot = lax.rem(z + rows - 1 + 2 * lax.rem(r_at, 2), turn)
+        return (spot // rows) * half + member, lax.rem(spot, rows)
+
+    def start_relay(t):
+        return upper * half + 2 * t + core, r_at
+
+    def proxy_of(side, row):
+        return half - 4 + 7 * side, row
+
+    proxy = f_at == proxy_of(upper, r_at)[0]
+    next_relay = relays_of(z_at, place)
+    last_to = (half - 1 + core, began)
     edge = far_up.astype(jnp.int32)
     beyond = 3 * edge
     flip = far_down.astype(jnp.int32)
@@ -82,8 +102,13 @@
 
     @pl.when(far)
     def _():
-        greet(jnp.where(far_up, half - 1 - spread, half + spread), r_at, x_at)
-        greet(jnp.where(far_up, half + spread, half - 1 - spread), r_at, x_at)
+        greet(*proxy_of(1 - upper, r_at), x_at)
+        for t in range(4):
+            greet(*relays_of(z_at + rows, 2 * t + 1 - core), x_at)
+
+    pl.when(both(first_relay, near))(lambda: greet(half - 1 + upper, r_at, x_at))
+    pl.when(first_relay)(lambda: greet(*proxy_of(upper, r_at), x_at))
+    pl.when(second_relay)(lambda: greet(*proxy_of(1 - core, began), x_at))
 
     @pl.when(jnp.logical_not(left))
     def _():
@@ -191,14 +216,54 @@
         )
 
     def tell():
-        pair_at = jnp.where(proxy_up, half - 1, half)
-        pl.semaphore_signal(ready, inc=1, device_id=(pair_at, r_at, x_at), device_id_type=MESH)
+        for t in range(4):
+            there = (upper * half + 2 * t + 1 - core, r_at, x_at)
+            pl.semaphore_signal(ready, inc=1, device_id=there, device_id_type=MESH)
+
+    def leg_one(t):
+        return hop(
+            block(t, edge + 1, 1), relay.at[0], leg_send.at[t], leg_recv.at[0], *start_relay(t)
+        )
+
+    def leg_two(src):
+        return hop(src, relay.at[1], leg_send.at[4], leg_recv.at[1], *next_relay)
+
+    def leg_three(t):
+        side = 1 - core
+        return hop(
+            relay.at[1], block(t, 3 * side, 1), leg_send.at[5], c_recv.at[t, side], *last_to
+        )
 
     def first_halo(t):
+        if t < 4:
+            pl.when(both(far, column != t))(lambda: leg_one(t).start())
         pl.when(right)(lambda: to_right(t).start())
         pl.when(left)(lambda: to_left(t).start())
         pl.when(near_up)(lambda: to_up(t).start())
         pl.when(near_down)(lambda: to_down(t).start())
+
+    def relay_one():
+        for t in range(4):
+            here = both(first_relay, column == t)
+
+            @pl.when(both(here, near))
+            def _():
+                leg_one(t).wait_recv()
+                pl.semaphore_wait(ready, 1)
+                leg_two(relay.at[0]).start()
+
+            @pl.when(both(here, far))
+            def _():
+                pl.semaphore_wait(ready, 1)
+                leg_two(block(t, edge + 1, 1)).start()
+
+    def relay_two(group):
+        for t in range(4):
+
+            @pl.when(both(group, both(second_relay, column == t)))
+            def _():
+                leg_two(relay.at[0]).wait_recv()
+                leg_three(t).start()
 
     def summary(side):
         there = jnp.where(far_up, half, half - 1)
@@ -254,9 +319,10 @@
                 high_halo(t)
 
     def halo_sent(t):
-        out_up, out_down = (up, down) if t < 4 else (near_up, near_down)
-        pl.when(out_up)(lambda: to_up(t).wait_send())
-        pl.when(out_down)(lambda: to_down(t).wait_send())
+        if t < 4:
+            pl.when(both(far, column != t))(lambda: leg_one(t).wait_send())
+        pl.when(near_up)(lambda: to_up(t).wait_send())
+        pl.when(near_down)(lambda: to_down(t).wait_send())
         pl.when(right)(lambda: to_right(t).wait_send())
         pl.when(left)(lambda: to_left(t).wait_send())
         pl.when(both(near_up, left))(lambda: side_up(t, 0).wait_send())
@@ -313,8 +379,10 @@
             moved = nn(to_heads, land[t, pl.ds(g * tall, tall)]).astype(jnp.bfloat16)
             pack[t, :, g // 2, pl.ds(16 * (g % 2), 16)] = moved.reshape(heads_all, 16, 128)
         if t == 0:
-            known = [right, left, near_up, near_down, proxy, proxy]
-            pl.semaphore_wait(barrier, heads - 1 + sum(c.astype(jnp.int32) for c in known))
+            known = [right, left, near_up, near_down, second_relay]
+            count = heads - 1 + sum(c.astype(jnp.int32) for c in known)
+            count += 3 * far.astype(jnp.int32) + 9 * proxy.astype(jnp.int32)
+            pl.semaphore_wait(barrier, count)
             pl.when(proxy)(tell)
         for k in range(1, heads):
             exchange(t, k).start()
@@ -336,16 +404,6 @@
     second_halo(VAL)
     gathered(GRD)
     first_halo(GRD)
-
-    @pl.when(far)
-    def _():
-        pl.semaphore_wait(ready, 1)
-        for t in range(4):
-            pl.when(far_up)(lambda: to_up(t).start())
-            pl.when(far_down)(lambda: to_down(t).start())
-
-    second_halo(QRY)
-    second_halo(GRD)
 
     lane_grid = lax.broadcasted_iota(jnp.int32, (128, 128), 1)
     power = scaling * math.log2(math.e)
@@ -471,14 +529,18 @@
                 land[o, span] = nn(to_rows, piece).astype(jnp.bfloat16)
             storing(o, half_at).start()
 
+    @pl.when(far)
+    def _():
+        lax.fori_loop(0, groups, near_step, 0)
+
+    second_halo(QRY)
+    relay_one()
+    pl.when(far)(lambda: summary(0).start())
+    second_halo(GRD)
     early_halo(KEY, VAL)
     lax.fori_loop(0, groups, query_step, 0)
     give(0, 0, 1)
-
-    @pl.when(far)
-    def _():
-        lax.fori_loop(0, groups, near_step, 0)
-        summary(0).start()
+    relay_two(far)
 
     for t in range(4):
         far_halo(t)
@@ -493,6 +555,7 @@
     lax.fori_loop(groups, groups * 2, query_step, 0)
     first_halo(4)
     give(1, 0, 1)
+    relay_two(near)
     finish(0, 0, 1)
     second_halo(4)
     early_halo(QRY, GRD, 4)
@@ -513,6 +576,8 @@
     for t in range(5):
         halo_sent(t)
     pl.when(far)(lambda: summary(0).wait_send())
+    pl.when(first_relay)(lambda: leg_two(relay.at[0]).wait_send())
+    pl.when(second_relay)(lambda: leg_three(0).wait_send())
     for o in range(4):
         storing(o, 0).wait()
         storing(o, 1).wait()
@@ -551,6 +616,7 @@
             pltpu.VMEM((2, 2, 1, 9 * 128), jnp.float32),
             pltpu.VMEM((2, 2, 1, 9 * 128), jnp.float32),
             pltpu.VMEM((6, 1, 128), jnp.float32),
+            pltpu.VMEM((2, groups) + block, jnp.bfloat16),
             pltpu.SMEM((3,) + table.shape[1:], jnp.int32),
             dma((4,)),
             dma((4, kinds)),
@@ -566,10 +632,12 @@
             dma((4, 2)),
             dma((2,)),
             dma((3,)),
+            dma((6,)),
+            dma((2,)),
             pltpu.SemaphoreType.REGULAR,
         ],
         compiler_params=pltpu.CompilerParams(
-            collective_id=0, has_side_effects=True, vmem_limit_bytes=48 << 20
+            collective_id=0, has_side_effects=True, vmem_limit_bytes=VMEM
         ),
     )(table, flat(keys), flat(values), flat(queries), flat(out_grad))
     return tuple(unflat(r) for r in results)

time: 112 us -> 91.7 us (0.82)
  Pallas kernels: 104 us -> 86.3 us
  local copies, waits for them, and re-layouts: 7.42 us -> 4.39 us
    pallas_call x1, Pallas kernels: 104 us -> 86.3 us  [on_device(): pl.pallas_call(functools.partial(tile_kernel, sizes), out_shape=[jax.Shap...]
    unnamed x14 -> x10, local copies, waits for them, and re-layouts: 7.42 us -> 4.39 us
where the time goes in v4:
time: 91.7 us; the launch traced here: 91.4 us
  Pallas kernels  86.3 us (94%)
  local copies, waits for them, and re-layouts  4.39 us (5%)
    pallas_call x1, Pallas kernels, on_device(): pl.pallas_call(functools.partial(tile_kernel, sizes), out_shape=[jax.Shap...  86.3 us
    unnamed x10, local copies, waits for them, and re-layouts  4.39 us

profile of v4, /device:TPU:25, one launch (start us, length us, event | category | flops | bytes accessed | tf_op | source)
XLA Modules:
  0.0 91.4 jit_solution(17372272745653080192)
XLA Ops:
  0.6 86.3 %shard_map.84 = (bf16[768,128]{1,0:T(8,128)(2,1)}, bf16[768,128]{1,0:T(8,128)(2,1)}, bf16[768,128]{1,0:T(8,128)(2,1)}, bf16[768,128]{1,0:T(8,128)(2,1)}) custom-call(s32[16,27,2,32]{3,2,1,0:T(2,128)} %bitcast.25, bf16[768,128]{1,0:T(8,128)(2,1)} %bitcast.26, bf16[768,128]{1,0:T(8,128)(2,1)} %bitcast.27, bf16[768,128]{1,0:T(8,128)(2,1)} %bitcast.28, ...), custom_call_target="tpu_custom_call" | custom-call | tf_op jit(solution)/shard_map/pallas_call | solution.py:603
  87.0 0.0 copy-start.2
  87.0 1.7 %copy.13 = bf16[2,8,4,12,128]{4,2,3,1,0:T(4,128)(2,1)} copy(bf16[2,8,4,12,128]{4,2,3,1,0:T(4,128)(2,1)} %bitcast.33) | data formatting | bytes 393216
  88.7 0.0 copy-done.2
  88.7 0.0 copy-start.1
  88.7 0.7 copy.14
  89.4 0.3 copy-done.1
  89.7 0.0 copy-start
  89.7 0.7 copy.15
  90.4 0.3 copy-done
  90.7 0.7 copy.16
Async XLA Ops:
  87.0 1.7 %copy-start.2 = (bf16[768,128]{1,0:T(8,128)(2,1)S(1)}, bf16[768,128]{1,0:T(8,128)(2,1)}, u32[]{:S(2)}) copy-start(bf16[768,128]{1,0:T(8,128)(2,1)} %get-tuple-element.9) | copy-start | bytes 589828
  88.7 1.0 %copy-start.1 = (bf16[768,128]{1,0:T(8,128)(2,1)S(1)}, bf16[768,128]{1,0:T(8,128)(2,1)}, u32[]{:S(2)}) copy-start(bf16[768,128]{1,0:T(8,128)(2,1)} %get-tuple-element.10) | copy-start | bytes 589828
  89.7 1.0 %copy-start = (bf16[768,128]{1,0:T(8,128)(2,1)S(1)}, bf16[768,128]{1,0:T(8,128)(2,1)}, u32[]{:S(2)}) copy-start(bf16[768,128]{1,0:T(8,128)(2,1)} %get-tuple-element.11) | copy-start | bytes 589828

commit v5 on v4

--- a/solution.py
+++ b/solution.py
@@ -27,9 +27,9 @@
 def tile_kernel(sizes, act_in, k_in, v_in, q_in, g_in, *refs):
     frames, rows, heads, groups, scaling = sizes
     outs, refs = refs[:4], refs[4:]
-    land, pack, wide, stats, own, back, part, front, behind, across, relay, act = refs[:12]
-    in_sem, a_send, a_recv, z_send, z_recv, c_send, c_recv, d_send, d_recv = refs[12:21]
-    o_send, o_recv, out_sem, part_sem, act_sem, leg_send, leg_recv, ready = refs[21:29]
+    land, pack, wide, stats, own, part, front, behind, across, relay, act = refs[:11]
+    in_sem, a_send, a_recv, z_send, z_recv, c_send, c_recv, d_send, d_recv = refs[11:20]
+    o_send, o_recv, out_sem, part_sem, act_sem, leg_send, leg_recv, ready = refs[20:28]
     ins = (k_in, v_in, q_in, g_in)
     heads_all = groups * heads
     tall = heads_all * 16
@@ -56,8 +56,8 @@
     second_relay = both(began >= 0, began < rows) & (lax.rem(began + turn, 2) == 1 - odd)
     near = jnp.logical_not(far)
 
-    def relays_of(z, member):
-        spot = lax.rem(z + rows - 1 + 2 * lax.rem(r_at, 2), turn)
+    def relays_of(z, row, member):
+        spot = lax.rem(z + rows - 1 + 2 * lax.rem(row, 2), turn)
         return (spot // rows) * half + member, lax.rem(spot, rows)
 
     def start_relay(t):
@@ -67,8 +67,8 @@
         return half - 4 + 7 * side, row
 
     proxy = f_at == proxy_of(upper, r_at)[0]
-    next_relay = relays_of(z_at, place)
-    last_to = (half - 1 + core, began)
+    next_relay = relays_of(z_at, r_at, place)
+    targets = [both(second_relay, both(began + 1 - v >= 0, began + 1 - v < rows)) for v in range(3)]
     edge = far_up.astype(jnp.int32)
     beyond = 3 * edge
     flip = far_down.astype(jnp.int32)
@@ -103,8 +103,13 @@
     @pl.when(far)
     def _():
         greet(*proxy_of(1 - upper, r_at), x_at)
-        for t in range(4):
-            greet(*relays_of(z_at + rows, 2 * t + 1 - core), x_at)
+        for v, known in enumerate((left, f_at >= 0, right)):
+
+            @pl.when(known)
+            def _():
+                for t in range(4):
+                    z, row = z_at + rows + v - 1, r_at + v - 1
+                    greet(*relays_of(z, row, 2 * t + 1 - core), x_at)
 
     pl.when(both(first_relay, near))(lambda: greet(half - 1 + upper, r_at, x_at))
     pl.when(first_relay)(lambda: greet(*proxy_of(upper, r_at), x_at))
@@ -137,7 +142,6 @@
         return ((row % 16) // 4) * (4 * heads_all) + (row // 16) * 4 + row % 4
 
     to_heads = (swapped(out_row) == in_row).astype(jnp.bfloat16)
-    to_rows = (swapped(in_row) == out_row).astype(jnp.bfloat16)
 
     def exchange(t, k):
         there = peers[k]
@@ -220,27 +224,46 @@
             there = (upper * half + 2 * t + 1 - core, r_at, x_at)
             pl.semaphore_signal(ready, inc=1, device_id=there, device_id_type=MESH)
 
-    def leg_one(t):
+    def leg_one(t, h):
         return hop(
-            block(t, edge + 1, 1), relay.at[0], leg_send.at[t], leg_recv.at[0], *start_relay(t)
-        )
-
-    def leg_two(src):
-        return hop(src, relay.at[1], leg_send.at[4], leg_recv.at[1], *next_relay)
-
-    def leg_three(t):
+            wide.at[t, h, edge + 1, 1],
+            relay.at[0, h],
+            leg_send.at[t * groups + h],
+            leg_recv.at[0, h],
+            *start_relay(t),
+        )
+
+    def leg_two(src, h):
+        return hop(
+            src, relay.at[1, h], leg_send.at[4 * groups + h], leg_recv.at[1, h], *next_relay
+        )
+
+    def leg_three(t, h, v):
         side = 1 - core
+        sem = c_recv.at[t, side] if v == 1 else d_recv.at[t, 2 * side + v // 2]
         return hop(
-            relay.at[1], block(t, 3 * side, 1), leg_send.at[5], c_recv.at[t, side], *last_to
+            relay.at[1, h],
+            wide.at[t, h, 3 * side, v],
+            leg_send.at[(5 + v) * groups + h],
+            sem,
+            half - 1 + core,
+            began + 1 - v,
         )
 
     def first_halo(t):
         if t < 4:
-            pl.when(both(far, column != t))(lambda: leg_one(t).start())
+
+            @pl.when(both(far, column != t))
+            def _():
+                for h in range(groups):
+                    leg_one(t, h).start()
+
+        pl.when(near_up)(lambda: to_up(t).start())
+        pl.when(near_down)(lambda: to_down(t).start())
+
+    def row_halo(t):
         pl.when(right)(lambda: to_right(t).start())
         pl.when(left)(lambda: to_left(t).start())
-        pl.when(near_up)(lambda: to_up(t).start())
-        pl.when(near_down)(lambda: to_down(t).start())
 
     def relay_one():
         for t in range(4):
@@ -248,22 +271,29 @@
 
             @pl.when(both(here, near))
             def _():
-                leg_one(t).wait_recv()
-                pl.semaphore_wait(ready, 1)
-                leg_two(relay.at[0]).start()
+                for h in range(groups):
+                    leg_one(t, h).wait_recv()
+                    if h == 0:
+                        pl.semaphore_wait(ready, 1)
+                    leg_two(relay.at[0, h], h).start()
 
             @pl.when(both(here, far))
             def _():
                 pl.semaphore_wait(ready, 1)
-                leg_two(block(t, edge + 1, 1)).start()
+                for h in range(groups):
+                    leg_two(wide.at[t, h, edge + 1, 1], h).start()
 
     def relay_two(group):
         for t in range(4):
-
-            @pl.when(both(group, both(second_relay, column == t)))
-            def _():
-                leg_two(relay.at[0]).wait_recv()
-                leg_three(t).start()
+            for h in range(groups):
+                here = both(group, column == t)
+
+                @pl.when(both(here, second_relay))
+                def _():
+                    leg_two(relay.at[0, h], h).wait_recv()
+
+                for v in (1, 0, 2):
+                    pl.when(both(here, targets[v]))(lambda: leg_three(t, h, v).start())
 
     def summary(side):
         there = jnp.where(far_up, half, half - 1)
@@ -281,10 +311,11 @@
         if t < 4:
             pl.when(far_down)(lambda: to_up(t).wait_recv())
             pl.when(far_up)(lambda: to_down(t).wait_recv())
-        pl.when(both(far_down, right))(lambda: along_right(t, 0).start())
-        pl.when(both(far_down, left))(lambda: along_left(t, 0).start())
-        pl.when(both(far_up, right))(lambda: along_right(t, 3).start())
-        pl.when(both(far_up, left))(lambda: along_left(t, 3).start())
+        if t == 4:
+            pl.when(both(far_down, right))(lambda: along_right(t, 0).start())
+            pl.when(both(far_down, left))(lambda: along_left(t, 0).start())
+            pl.when(both(far_up, right))(lambda: along_right(t, 3).start())
+            pl.when(both(far_up, left))(lambda: along_left(t, 3).start())
 
     def low_halo(t):
         pl.when(near_down)(lambda: to_up(t).wait_recv())
@@ -320,7 +351,12 @@
 
     def halo_sent(t):
         if t < 4:
-            pl.when(both(far, column != t))(lambda: leg_one(t).wait_send())
+
+            @pl.when(both(far, column != t))
+            def _():
+                for h in range(groups):
+                    leg_one(t, h).wait_send()
+
         pl.when(near_up)(lambda: to_up(t).wait_send())
         pl.when(near_down)(lambda: to_down(t).wait_send())
         pl.when(right)(lambda: to_right(t).wait_send())
@@ -329,10 +365,11 @@
         pl.when(both(near_up, right))(lambda: side_up(t, 2).wait_send())
         pl.when(both(near_down, left))(lambda: side_down(t, 0).wait_send())
         pl.when(both(near_down, right))(lambda: side_down(t, 2).wait_send())
-        pl.when(both(far_down, right))(lambda: along_right(t, 0).wait_send())
-        pl.when(both(far_down, left))(lambda: along_left(t, 0).wait_send())
-        pl.when(both(far_up, right))(lambda: along_right(t, 3).wait_send())
-        pl.when(both(far_up, left))(lambda: along_left(t, 3).wait_send())
+        if t == 4:
+            pl.when(both(far_down, right))(lambda: along_right(t, 0).wait_send())
+            pl.when(both(far_down, left))(lambda: along_left(t, 0).wait_send())
+            pl.when(both(far_up, right))(lambda: along_right(t, 3).wait_send())
+            pl.when(both(far_up, left))(lambda: along_left(t, 3).wait_send())
 
     for j in range(3):
         loading_act(j).wait()
@@ -379,7 +416,7 @@
             moved = nn(to_heads, land[t, pl.ds(g * tall, tall)]).astype(jnp.bfloat16)
             pack[t, :, g // 2, pl.ds(16 * (g % 2), 16)] = moved.reshape(heads_all, 16, 128)
         if t == 0:
-            known = [right, left, near_up, near_down, second_relay]
+            known = [right, left, near_up, near_down] + targets
             count = heads - 1 + sum(c.astype(jnp.int32) for c in known)
             count += 3 * far.astype(jnp.int32) + 9 * proxy.astype(jnp.int32)
             pl.semaphore_wait(barrier, count)
@@ -396,8 +433,10 @@
 
     gathered(KEY)
     first_halo(KEY)
+    row_halo(KEY)
     gathered(VAL)
     first_halo(VAL)
+    row_halo(VAL)
     second_halo(KEY)
     gathered(QRY)
     first_halo(QRY)
@@ -486,7 +525,7 @@
         spot = pl.ds(pl.multiple_of(peers[k] * 32, 32), 32)
         return pltpu.make_async_remote_copy(
             src_ref=own.at[o, :, f, spot],
-            dst_ref=back.at[o, pl.ds(x_at * groups, groups), f],
+            dst_ref=outs[o].at[pl.ds(x_at * groups, groups), f],
             send_sem=o_send.at[o, half_at, k - 1],
             recv_sem=o_recv.at[o, half_at, k - 1],
             device_id=(f_at, r_at, peers[k]),
@@ -497,7 +536,7 @@
         f = half_at ^ flip
         return pltpu.make_async_remote_copy(
             src_ref=own.at[o, :, f, pl.ds(0, 32)],
-            dst_ref=back.at[o, pl.ds(froms[k] * groups, groups), f],
+            dst_ref=outs[o].at[pl.ds(froms[k] * groups, groups), f],
             send_sem=o_send.at[o, half_at, k - 1],
             recv_sem=o_recv.at[o, half_at, k - 1],
             device_id=(f_at, r_at, froms[k]),
@@ -509,38 +548,35 @@
         for o in kinds:
             for k in range(1, heads):
                 giving(o, half_at, k).start()
-        for o in kinds:
-            spot = pl.ds(pl.multiple_of(x_at * 32, 32), 32)
-            back[o, pl.ds(x_at * groups, groups), f] = own[o, :, f, spot]
-
-    def storing(o, half_at):
+            keeping(o, half_at).start()
+
+    def keeping(o, half_at):
         f = half_at ^ flip
-        span = pl.ds(pl.multiple_of(f * 2 * tall, 2 * tall), 2 * tall)
-        return pltpu.make_async_copy(land.at[o, span], outs[o].at[span], out_sem.at[o, half_at])
-
-    def finish(half_at, *kinds):
-        f = half_at ^ flip
-        for o in kinds:
-            for k in range(1, heads):
-                taking(o, half_at, k).wait_recv()
-            for g in range(2):
-                piece = back[o, :, f, pl.ds(16 * g, 16)].reshape(tall, 128)
-                span = pl.ds(pl.multiple_of((f * 2 + g) * tall, tall), tall)
-                land[o, span] = nn(to_rows, piece).astype(jnp.bfloat16)
-            storing(o, half_at).start()
+        spot = pl.ds(pl.multiple_of(x_at * 32, 32), 32)
+        return pltpu.make_async_copy(
+            own.at[o, :, f, spot],
+            outs[o].at[pl.ds(x_at * groups, groups), f],
+            out_sem.at[o, half_at],
+        )
+
+    relay_one()
 
     @pl.when(far)
     def _():
         lax.fori_loop(0, groups, near_step, 0)
 
-    second_halo(QRY)
-    relay_one()
     pl.when(far)(lambda: summary(0).start())
-    second_halo(GRD)
     early_halo(KEY, VAL)
+    row_halo(QRY)
+    row_halo(GRD)
     lax.fori_loop(0, groups, query_step, 0)
     give(0, 0, 1)
     relay_two(far)
+
+    @pl.when(far)
+    def _():
+        second_halo(QRY)
+        second_halo(GRD)
 
     for t in range(4):
         far_halo(t)
@@ -554,19 +590,22 @@
     late_halo(KEY, VAL)
     lax.fori_loop(groups, groups * 2, query_step, 0)
     first_halo(4)
+    row_halo(4)
+
+    @pl.when(near)
+    def _():
+        second_halo(QRY)
+        second_halo(GRD)
+
     give(1, 0, 1)
     relay_two(near)
-    finish(0, 0, 1)
     second_halo(4)
     early_halo(QRY, GRD, 4)
     lax.fori_loop(0, groups, key_step, 0)
     give(0, 2, 3)
-    finish(1, 0, 1)
     late_halo(QRY, GRD, 4)
     lax.fori_loop(groups, groups * 2, key_step, 0)
     give(1, 2, 3)
-    finish(0, 2, 3)
-    finish(1, 2, 3)
 
     for t in range(4):
         for k in range(1, heads):
@@ -576,11 +615,15 @@
     for t in range(5):
         halo_sent(t)
     pl.when(far)(lambda: summary(0).wait_send())
-    pl.when(first_relay)(lambda: leg_two(relay.at[0]).wait_send())
-    pl.when(second_relay)(lambda: leg_three(0).wait_send())
+    for h in range(groups):
+        pl.when(first_relay)(lambda: leg_two(relay.at[0, h], h).wait_send())
+        for v in range(3):
+            pl.when(targets[v])(lambda: leg_three(0, h, v).wait_send())
     for o in range(4):
-        storing(o, 0).wait()
-        storing(o, 1).wait()
+        for half_at in range(2):
+            keeping(o, half_at).wait()
+            for k in range(1, heads):
+                taking(o, half_at, k).wait_recv()
 
 
 def on_device(sizes, queries, keys, values, out_grad, active):
@@ -593,8 +636,8 @@
         return jnp.transpose(tensor, (0, 1, 3, 2, 4)).reshape(tall, head_dim)
 
     def unflat(tensor):
-        shaped = tensor.reshape(frames_here, rows_here, heads_all, cols_here, head_dim)
-        return jnp.transpose(shaped, (0, 1, 3, 2, 4))
+        shaped = tensor.reshape(heads_all, frames_here, rows_here, cols_here, head_dim)
+        return jnp.transpose(shaped, (1, 2, 3, 0, 4))
 
     dma = pltpu.SemaphoreType.DMA
     block = (128, head_dim)
@@ -602,7 +645,7 @@
     anywhere = pl.BlockSpec(memory_space=pl.ANY)
     results = pl.pallas_call(
         functools.partial(tile_kernel, sizes),
-        out_shape=[jax.ShapeDtypeStruct((tall, head_dim), jnp.bfloat16)] * 4,
+        out_shape=[jax.ShapeDtypeStruct((heads_all, 2, 32, head_dim), jnp.bfloat16)] * 4,
         in_specs=[anywhere] * 5,
         out_specs=[anywhere] * 4,
         scratch_shapes=[
@@ -611,7 +654,6 @@
             pltpu.VMEM((4, groups, 4, 3) + block, jnp.bfloat16),
             pltpu.VMEM((groups, 4, 3, 8, 128), jnp.float32),
             pltpu.VMEM((4, groups, 2) + block, jnp.bfloat16),
-            pltpu.VMEM((4, heads_all, 2, 32, head_dim), jnp.bfloat16),
             pltpu.VMEM((2, groups, 8, 128), jnp.float32),
             pltpu.VMEM((2, 2, 1, 9 * 128), jnp.float32),
             pltpu.VMEM((2, 2, 1, 9 * 128), jnp.float32),
@@ -632,8 +674,8 @@
             dma((4, 2)),
             dma((2,)),
             dma((3,)),
-            dma((6,)),
-            dma((2,)),
+            dma((8 * groups,)),
+            dma((2, groups)),
             pltpu.SemaphoreType.REGULAR,
         ],
         compiler_params=pltpu.CompilerParams(

time: 91.7 us -> 84.6 us (0.923)
  Pallas kernels: 86.3 us -> 80.4 us
  local copies, waits for them, and re-layouts: 4.39 us -> 2.84 us
    pallas_call x1, Pallas kernels: 86.3 us -> 80.4 us  [on_device(): pl.pallas_call(functools.partial(tile_kernel, sizes), out_shape=[jax.Shap...]
    unnamed x10 -> x4, local copies, waits for them, and re-layouts: 4.39 us -> 0.01 us
    transpose x0 -> x2, local copies, waits for them, and re-layouts: none -> 2.83 us  [unflat(): return jnp.transpose(shaped, (1, 2, 3, 0, 4))]
where the time goes in v5:
time: 84.6 us; the launch traced here: 83.9 us
  Pallas kernels  80.4 us (95%)
  local copies, waits for them, and re-layouts  2.84 us (3%)
    pallas_call x1, Pallas kernels, on_device(): pl.pallas_call(functools.partial(tile_kernel, sizes), out_shape=[jax.Shap...  80.4 us
    transpose x2, local copies, waits for them, and re-layouts, unflat(): return jnp.transpose(shaped, (1, 2, 3, 0, 4))  2.83 us

profile of v5, /device:TPU:25, one launch (start us, length us, event | category | flops | bytes accessed | tf_op | source)
XLA Modules:
  0.0 83.9 jit_solution(17949835517692316240)
XLA Ops:
  0.6 80.4 %shard_map.84 = (bf16[12,2,32,128]{3,2,1,0:T(8,128)(2,1)}, bf16[12,2,32,128]{3,2,1,0:T(8,128)(2,1)}, bf16[12,2,32,128]{3,2,1,0:T(8,128)(2,1)}, bf16[12,2,32,128]{3,2,1,0:T(8,128)(2,1)}) custom-call(s32[16,27,2,32]{3,2,1,0:T(2,128)} %bitcast.25, bf16[768,128]{1,0:T(8,128)(2,1)} %bitcast.26, bf16[768,128]{1,0:T(8,128)(2,1)} %bitcast.27, ...), custom_call_target="tpu_custom_call" | custom-call | tf_op jit(solution)/shard_map/pallas_call | solution.py:646
  81.1 0.0 copy-start
  81.1 0.0 copy-start.1
  81.1 1.9 %copy_bitcast_fusion.2 = (bf16[2,8,4,12,128]{4,2,3,1,0:T(4,128)(2,1)}, bf16[2,8,4,12,128]{4,2,3,1,0:T(4,128)(2,1)}) fusion(bf16[12,2,8,4,128]{4,3,2,1,0:T(4,128)(2,1)} %bitcast.33, bf16[12,2,8,4,128]{4,3,2,1,0:T(4,128)(2,1)} %bitcast.32), kind=kLoop, calls=%fused_computation.2 | loop fusion | bytes 786432 | tf_op jit(solution)/shard_map/transpose | solution.py:640
  83.0 0.0 copy-done
  83.0 0.0 copy-done.1
  83.0 0.9 %copy_bitcast_fusion = (bf16[2,8,4,12,128]{4,2,3,1,0:T(4,128)(2,1)}, bf16[2,8,4,12,128]{4,2,3,1,0:T(4,128)(2,1)}) fusion(bf16[12,2,8,4,128]{4,3,2,1,0:T(4,128)(2,1)S(1)} %bitcast.31, bf16[12,2,8,4,128]{4,3,2,1,0:T(4,128)(2,1)S(1)} %bitcast.30), kind=kLoop, calls=%fused_computation | loop fusion | bytes 786432 | tf_op jit(solution)/shard_map/transpose | solution.py:640
Async XLA Ops:
  81.1 2.0 %copy-start = (bf16[12,2,32,128]{3,2,1,0:T(8,128)(2,1)S(1)}, bf16[12,2,32,128]{3,2,1,0:T(8,128)(2,1)}, u32[]{:S(2)}) copy-start(bf16[12,2,32,128]{3,2,1,0:T(8,128)(2,1)} %get-tuple-element.10) | copy-start | bytes 589828
  81.1 2.0 %copy-start.1 = (bf16[12,2,32,128]{3,2,1,0:T(8,128)(2,1)S(1)}, bf16[12,2,32,128]{3,2,1,0:T(8,128)(2,1)}, u32[]{:S(2)}) copy-start(bf16[12,2,32,128]{3,2,1,0:T(8,128)(2,1)} %get-tuple-element.11) | copy-start | bytes 589828

commit v6 on v5

--- a/solution.py
+++ b/solution.py
@@ -55,6 +55,8 @@
     began = jnp.where(odd == 1, shifted - (rows - 1), lax.rem(shifted + turn - rows - 1, turn))
     second_relay = both(began >= 0, began < rows) & (lax.rem(began + turn, 2) == 1 - odd)
     near = jnp.logical_not(far)
+    soon = both(upper == 1, r_at < rows // 2)
+    later = jnp.logical_not(soon)
 
     def relays_of(z, row, member):
         spot = lax.rem(z + rows - 1 + 2 * lax.rem(row, 2), turn)
@@ -265,9 +267,9 @@
         pl.when(right)(lambda: to_right(t).start())
         pl.when(left)(lambda: to_left(t).start())
 
-    def relay_one():
-        for t in range(4):
-            here = both(first_relay, column == t)
+    def relay_one(group, *kinds):
+        for t in kinds:
+            here = both(group, both(first_relay, column == t))
 
             @pl.when(both(here, near))
             def _():
@@ -437,12 +439,15 @@
     gathered(VAL)
     first_halo(VAL)
     row_halo(VAL)
+    relay_one(soon, KEY)
     second_halo(KEY)
     gathered(QRY)
     first_halo(QRY)
+    relay_one(soon, VAL)
     second_halo(VAL)
     gathered(GRD)
     first_halo(GRD)
+    relay_one(soon, QRY, GRD)
 
     lane_grid = lax.broadcasted_iota(jnp.int32, (128, 128), 1)
     power = scaling * math.log2(math.e)
@@ -559,7 +564,7 @@
             out_sem.at[o, half_at],
         )
 
-    relay_one()
+    relay_one(later, KEY, VAL, QRY, GRD)
 
     @pl.when(far)
     def _():
@@ -571,22 +576,15 @@
     row_halo(GRD)
     lax.fori_loop(0, groups, query_step, 0)
     give(0, 0, 1)
-    relay_two(far)
+    relay_two(far_down)
 
     @pl.when(far)
     def _():
         second_halo(QRY)
         second_halo(GRD)
 
-    for t in range(4):
-        far_halo(t)
-
-    @pl.when(far)
-    def _():
-        summary(0).wait_recv()
-        lax.fori_loop(0, groups, across_step, 0)
-
-    far_halo(4)
+    far_halo(KEY)
+    far_halo(VAL)
     late_halo(KEY, VAL)
     lax.fori_loop(groups, groups * 2, query_step, 0)
     first_halo(4)
@@ -598,11 +596,20 @@
         second_halo(GRD)
 
     give(1, 0, 1)
-    relay_two(near)
+    relay_two(jnp.logical_not(far_down))
     second_halo(4)
     early_halo(QRY, GRD, 4)
     lax.fori_loop(0, groups, key_step, 0)
     give(0, 2, 3)
+    far_halo(QRY)
+    far_halo(GRD)
+
+    @pl.when(far)
+    def _():
+        summary(0).wait_recv()
+        lax.fori_loop(0, groups, across_step, 0)
+
+    far_halo(4)
     late_halo(QRY, GRD, 4)
     lax.fori_loop(groups, groups * 2, key_step, 0)
     give(1, 2, 3)

time: 84.6 us -> 80 us (0.946)
  Pallas kernels: 80.4 us -> 75.2 us
    pallas_call x1, Pallas kernels: 80.4 us -> 75.2 us  [on_device(): pl.pallas_call(functools.partial(tile_kernel, sizes), out_shape=[jax.Shap...]
where the time goes in v6:
time: 80 us; the launch traced here: 78.7 us
  Pallas kernels  75.2 us (94%)
  local copies, waits for them, and re-layouts  2.84 us (4%)
    pallas_call x1, Pallas kernels, on_device(): pl.pallas_call(functools.partial(tile_kernel, sizes), out_shape=[jax.Shap...  75.2 us
    transpose x2, local copies, waits for them, and re-layouts, unflat(): return jnp.transpose(shaped, (1, 2, 3, 0, 4))  2.83 us

profile of v6, /device:TPU:25, one launch (start us, length us, event | category | flops | bytes accessed | tf_op | source)
XLA Modules:
  0.0 78.7 jit_solution(1385772857150538099)
XLA Ops:
  0.6 75.2 %shard_map.84 = (bf16[12,2,32,128]{3,2,1,0:T(8,128)(2,1)}, bf16[12,2,32,128]{3,2,1,0:T(8,128)(2,1)}, bf16[12,2,32,128]{3,2,1,0:T(8,128)(2,1)}, bf16[12,2,32,128]{3,2,1,0:T(8,128)(2,1)}) custom-call(s32[16,27,2,32]{3,2,1,0:T(2,128)} %bitcast.25, bf16[768,128]{1,0:T(8,128)(2,1)} %bitcast.26, bf16[768,128]{1,0:T(8,128)(2,1)} %bitcast.27, ...), custom_call_target="tpu_custom_call" | custom-call | tf_op jit(solution)/shard_map/pallas_call | solution.py:653
  75.8 0.0 copy-start
  75.9 0.0 copy-start.1
  75.9 1.9 %copy_bitcast_fusion.2 = (bf16[2,8,4,12,128]{4,2,3,1,0:T(4,128)(2,1)}, bf16[2,8,4,12,128]{4,2,3,1,0:T(4,128)(2,1)}) fusion(bf16[12,2,8,4,128]{4,3,2,1,0:T(4,128)(2,1)} %bitcast.33, bf16[12,2,8,4,128]{4,3,2,1,0:T(4,128)(2,1)} %bitcast.32), kind=kLoop, calls=%fused_computation.2 | loop fusion | bytes 786432 | tf_op jit(solution)/shard_map/transpose | solution.py:647
  77.8 0.0 copy-done
  77.8 0.0 copy-done.1
  77.8 0.9 %copy_bitcast_fusion = (bf16[2,8,4,12,128]{4,2,3,1,0:T(4,128)(2,1)}, bf16[2,8,4,12,128]{4,2,3,1,0:T(4,128)(2,1)}) fusion(bf16[12,2,8,4,128]{4,3,2,1,0:T(4,128)(2,1)S(1)} %bitcast.31, bf16[12,2,8,4,128]{4,3,2,1,0:T(4,128)(2,1)S(1)} %bitcast.30), kind=kLoop, calls=%fused_computation | loop fusion | bytes 786432 | tf_op jit(solution)/shard_map/transpose | solution.py:647
Async XLA Ops:
  75.8 2.0 %copy-start = (bf16[12,2,32,128]{3,2,1,0:T(8,128)(2,1)S(1)}, bf16[12,2,32,128]{3,2,1,0:T(8,128)(2,1)}, u32[]{:S(2)}) copy-start(bf16[12,2,32,128]{3,2,1,0:T(8,128)(2,1)} %get-tuple-element.10) | copy-start | bytes 589828
  75.9 2.0 %copy-start.1 = (bf16[12,2,32,128]{3,2,1,0:T(8,128)(2,1)S(1)}, bf16[12,2,32,128]{3,2,1,0:T(8,128)(2,1)}, u32[]{:S(2)}) copy-start(bf16[12,2,32,128]{3,2,1,0:T(8,128)(2,1)} %get-tuple-element.11) | copy-start | bytes 589828

commit v7 on v6

--- a/solution.py
+++ b/solution.py
@@ -572,11 +572,21 @@
 
     pl.when(far)(lambda: summary(0).start())
     early_halo(KEY, VAL)
-    row_halo(QRY)
-    row_halo(GRD)
+
+    @pl.when(far)
+    def _():
+        row_halo(QRY)
+        row_halo(GRD)
+
     lax.fori_loop(0, groups, query_step, 0)
+    relay_two(far_down)
+
+    @pl.when(near)
+    def _():
+        row_halo(QRY)
+        row_halo(GRD)
+
     give(0, 0, 1)
-    relay_two(far_down)
 
     @pl.when(far)
     def _():

time: 80 us -> 81.4 us (1.018)
  Pallas kernels: 75.2 us -> 76.4 us
    pallas_call x1, Pallas kernels: 75.2 us -> 76.4 us  [on_device(): pl.pallas_call(functools.partial(tile_kernel, sizes), out_shape=[jax.Shap...]
where the time goes in v7:
time: 81.4 us; the launch traced here: 79.9 us
  Pallas kernels  76.4 us (94%)
  local copies, waits for them, and re-layouts  2.84 us (3%)
    pallas_call x1, Pallas kernels, on_device(): pl.pallas_call(functools.partial(tile_kernel, sizes), out_shape=[jax.Shap...  76.4 us
    transpose x2, local copies, waits for them, and re-layouts, unflat(): return jnp.transpose(shaped, (1, 2, 3, 0, 4))  2.83 us

profile of v7, /device:TPU:25, one launch (start us, length us, event | category | flops | bytes accessed | tf_op | source)
XLA Modules:
  0.0 79.9 jit_solution(14431898303476138132)
XLA Ops:
  0.6 76.4 %shard_map.84 = (bf16[12,2,32,128]{3,2,1,0:T(8,128)(2,1)}, bf16[12,2,32,128]{3,2,1,0:T(8,128)(2,1)}, bf16[12,2,32,128]{3,2,1,0:T(8,128)(2,1)}, bf16[12,2,32,128]{3,2,1,0:T(8,128)(2,1)}) custom-call(s32[16,27,2,32]{3,2,1,0:T(2,128)} %bitcast.25, bf16[768,128]{1,0:T(8,128)(2,1)} %bitcast.26, bf16[768,128]{1,0:T(8,128)(2,1)} %bitcast.27, ...), custom_call_target="tpu_custom_call" | custom-call | tf_op jit(solution)/shard_map/pallas_call | solution.py:663
  77.0 0.0 copy-start
  77.0 0.0 copy-start.1
  77.0 1.9 %copy_bitcast_fusion.2 = (bf16[2,8,4,12,128]{4,2,3,1,0:T(4,128)(2,1)}, bf16[2,8,4,12,128]{4,2,3,1,0:T(4,128)(2,1)}) fusion(bf16[12,2,8,4,128]{4,3,2,1,0:T(4,128)(2,1)} %bitcast.33, bf16[12,2,8,4,128]{4,3,2,1,0:T(4,128)(2,1)} %bitcast.32), kind=kLoop, calls=%fused_computation.2 | loop fusion | bytes 786432 | tf_op jit(solution)/shard_map/transpose | solution.py:657
  79.0 0.0 copy-done
  79.0 0.0 copy-done.1
  79.0 0.9 %copy_bitcast_fusion = (bf16[2,8,4,12,128]{4,2,3,1,0:T(4,128)(2,1)}, bf16[2,8,4,12,128]{4,2,3,1,0:T(4,128)(2,1)}) fusion(bf16[12,2,8,4,128]{4,3,2,1,0:T(4,128)(2,1)S(1)} %bitcast.31, bf16[12,2,8,4,128]{4,3,2,1,0:T(4,128)(2,1)S(1)} %bitcast.30), kind=kLoop, calls=%fused_computation | loop fusion | bytes 786432 | tf_op jit(solution)/shard_map/transpose | solution.py:657
Async XLA Ops:
  77.0 2.0 %copy-start = (bf16[12,2,32,128]{3,2,1,0:T(8,128)(2,1)S(1)}, bf16[12,2,32,128]{3,2,1,0:T(8,128)(2,1)}, u32[]{:S(2)}) copy-start(bf16[12,2,32,128]{3,2,1,0:T(8,128)(2,1)} %get-tuple-element.10) | copy-start | bytes 589828
  77.0 2.0 %copy-start.1 = (bf16[12,2,32,128]{3,2,1,0:T(8,128)(2,1)S(1)}, bf16[12,2,32,128]{3,2,1,0:T(8,128)(2,1)}, u32[]{:S(2)}) copy-start(bf16[12,2,32,128]{3,2,1,0:T(8,128)(2,1)} %get-tuple-element.11) | copy-start | bytes 589828

commit v8 on v6

--- a/solution.py
+++ b/solution.py
@@ -448,6 +448,8 @@
     gathered(GRD)
     first_halo(GRD)
     relay_one(soon, QRY, GRD)
+    row_halo(QRY)
+    row_halo(GRD)
 
     lane_grid = lax.broadcasted_iota(jnp.int32, (128, 128), 1)
     power = scaling * math.log2(math.e)
@@ -572,8 +574,6 @@
 
     pl.when(far)(lambda: summary(0).start())
     early_halo(KEY, VAL)
-    row_halo(QRY)
-    row_halo(GRD)
     lax.fori_loop(0, groups, query_step, 0)
     give(0, 0, 1)
     relay_two(far_down)

time: 80 us -> 84.1 us (1.051)
  the two profiles are of different devices: /device:TPU:25 before, /device:TPU:217 now
where the time goes in v8:
time: 84.1 us; the launch traced here: 83.8 us
  Pallas kernels  80.3 us (95%)
  local copies, waits for them, and re-layouts  2.84 us (3%)
    pallas_call x1, Pallas kernels, on_device(): pl.pallas_call(functools.partial(tile_kernel, sizes), out_shape=[jax.Shap...  80.3 us
    transpose x2, local copies, waits for them, and re-layouts, unflat(): return jnp.transpose(shaped, (1, 2, 3, 0, 4))  2.83 us

profile of v8, /device:TPU:217, one launch (start us, length us, event | category | flops | bytes accessed | tf_op | source)
XLA Modules:
  0.0 83.8 jit_solution(16934282803509446077)
XLA Ops:
  0.6 80.3 %shard_map.84 = (bf16[12,2,32,128]{3,2,1,0:T(8,128)(2,1)}, bf16[12,2,32,128]{3,2,1,0:T(8,128)(2,1)}, bf16[12,2,32,128]{3,2,1,0:T(8,128)(2,1)}, bf16[12,2,32,128]{3,2,1,0:T(8,128)(2,1)}) custom-call(s32[16,27,2,32]{3,2,1,0:T(2,128)} %bitcast.25, bf16[768,128]{1,0:T(8,128)(2,1)} %bitcast.26, bf16[768,128]{1,0:T(8,128)(2,1)} %bitcast.27, ...), custom_call_target="tpu_custom_call" | custom-call | tf_op jit(solution)/shard_map/pallas_call | solution.py:653
  81.0 0.0 copy-start
  81.0 0.0 copy-start.1
  81.0 1.9 %copy_bitcast_fusion.2 = (bf16[2,8,4,12,128]{4,2,3,1,0:T(4,128)(2,1)}, bf16[2,8,4,12,128]{4,2,3,1,0:T(4,128)(2,1)}) fusion(bf16[12,2,8,4,128]{4,3,2,1,0:T(4,128)(2,1)} %bitcast.33, bf16[12,2,8,4,128]{4,3,2,1,0:T(4,128)(2,1)} %bitcast.32), kind=kLoop, calls=%fused_computation.2 | loop fusion | bytes 786432 | tf_op jit(solution)/shard_map/transpose | solution.py:647
  82.9 0.0 copy-done
  82.9 0.0 copy-done.1
  82.9 0.9 %copy_bitcast_fusion = (bf16[2,8,4,12,128]{4,2,3,1,0:T(4,128)(2,1)}, bf16[2,8,4,12,128]{4,2,3,1,0:T(4,128)(2,1)}) fusion(bf16[12,2,8,4,128]{4,3,2,1,0:T(4,128)(2,1)S(1)} %bitcast.31, bf16[12,2,8,4,128]{4,3,2,1,0:T(4,128)(2,1)S(1)} %bitcast.30), kind=kLoop, calls=%fused_computation | loop fusion | bytes 786432 | tf_op jit(solution)/shard_map/transpose | solution.py:647
Async XLA Ops:
  81.0 2.0 %copy-start = (bf16[12,2,32,128]{3,2,1,0:T(8,128)(2,1)S(1)}, bf16[12,2,32,128]{3,2,1,0:T(8,128)(2,1)}, u32[]{:S(2)}) copy-start(bf16[12,2,32,128]{3,2,1,0:T(8,128)(2,1)} %get-tuple-element.10) | copy-start | bytes 589828
  81.0 2.0 %copy-start.1 = (bf16[12,2,32,128]{3,2,1,0:T(8,128)(2,1)S(1)}, bf16[12,2,32,128]{3,2,1,0:T(8,128)(2,1)}, u32[]{:S(2)}) copy-start(bf16[12,2,32,128]{3,2,1,0:T(8,128)(2,1)} %get-tuple-element.11) | copy-start | bytes 589828
